TPU v7x, 256 devices: a whole 4x4x8 slice. The times are simulated.
256 devices in a mesh: dp: 32 (over z_hi, x, core), seq: 8 (over y, z_lo).
Axes of the slice: x: 4, y: 4, z: 8 (z_hi: 4, z_lo: 2; z = z_hi * 2 + z_lo), core: 2. Of those that a mesh axis runs over, the one named last changes fastest.
Arguments:
- q_proj: bfloat16 [32, 1024, 4096], P('dp', 'seq'), may hold values from -200 to 200
- k_proj: bfloat16 [32, 1024, 512], P('dp', 'seq'), may hold values from -6 to 6
- v_proj: bfloat16 [32, 1024, 512], P('dp', 'seq'), may hold values from -6 to 6
- cache_k: bfloat16 [32, 1024, 512], P('dp', 'seq'), may hold values from -6 to 6
- cache_v: bfloat16 [32, 1024, 512], P('dp', 'seq'), may hold values from -6 to 6
- bias_q: bfloat16 [4096], replicated, may hold values from -3 to 3
- bias_k: bfloat16 [512], replicated, may hold values from -3 to 3
- bias_v: bfloat16 [512], replicated, may hold values from -3 to 3
- start: int32 [32], P('dp'), may hold values from 256 to 1024, as said below
- dout: bfloat16 [32, 1024, 4096], P('dp', 'seq'), may hold values from -6 to 6
Outputs:
- attn_out: bfloat16 [32, 1024, 4096], P('dp', 'seq')
- grad_q: bfloat16 [32, 1024, 4096], P('dp', 'seq')
- grad_k: bfloat16 [32, 1024, 512], P('dp', 'seq')
- grad_v: bfloat16 [32, 1024, 512], P('dp', 'seq')
- grad_bias_q: float32 [4096], replicated
- grad_bias_k: float32 [512], replicated
- grad_bias_v: float32 [512], replicated
Inputs may be any that keep to these rules, and one draw needn't show every extreme that they name: Cache slots at and beyond start hold no prefix; some sequence has a full prefix of 1024 slots.
All inputs are finite; a program needn't handle non-finite values.
Results may differ from a plain program's by a relative error of at most 0.04.
The roundings to bfloat16 on the way count: a program that leaves them out, or rounds other values in their place, can miss the bound.
Values may be sent and summed in bfloat16 or wider, within the bound.
A program may use at most 128 MiB of HBM per device.

v0:
```python
import jax
import jax.numpy as jnp
from jax import lax
from jax.sharding import PartitionSpec as P

HQ = 32
KV = 4
HD = 128
GROUP = 8


def rotary_tables(positions, width):
    half = width // 2
    freqs = jnp.exp(
        -(2.0 * jnp.arange(half, dtype=jnp.float32) / width) * jnp.log(jnp.float32(1000000.0))
    )
    angles = positions.astype(jnp.float32)[:, None] * freqs[None, :]
    cosine = jnp.concatenate([jnp.cos(angles), jnp.cos(angles)], axis=1)
    sine = jnp.concatenate([jnp.sin(angles), jnp.sin(angles)], axis=1)
    return (cosine[:, None, :], sine[:, None, :])


def rotary(values, positions):
    cosine, sine = rotary_tables(positions, values.shape[2])
    half = values.shape[2] // 2
    turned = jnp.concatenate([-values[:, :, half:], values[:, :, :half]], axis=2)
    return values * cosine + turned * sine


def rotary_back(grads, positions):
    cosine, sine = rotary_tables(positions, grads.shape[2])
    half = grads.shape[2] // 2
    scaled = grads * sine
    turned = jnp.concatenate([scaled[:, :, half:], -scaled[:, :, :half]], axis=2)
    return grads * cosine + turned


def attend(queries, cotangent, keys, values, first, row_zero, prefix):
    rows, heads, width = queries.shape
    key_count = keys.shape[0]
    slab = key_count - prefix
    head_block = max(1, min(512 // rows, GROUP, heads))
    row_block = min(rows, 512)
    scale = width ** (-0.5)
    key_index = jnp.arange(key_count, dtype=jnp.int32)

    def head_step(carry, head_slot):
        key_acc, value_acc = carry
        head_zero = head_slot * head_block
        owner = head_zero // GROUP
        key_one = lax.dynamic_index_in_dim(keys, owner, 1, keepdims=False)
        value_one = lax.dynamic_index_in_dim(values, owner, 1, keepdims=False)
        query_part = lax.dynamic_slice_in_dim(queries, head_zero, head_block, 1)
        cot_part = lax.dynamic_slice_in_dim(cotangent, head_zero, head_block, 1)

        def row_step(inner, row_slot):
            grad_key, grad_value = inner
            offset = row_slot * row_block
            query_rows = lax.dynamic_slice_in_dim(query_part, offset, row_block, 0)
            cot_rows = lax.dynamic_slice_in_dim(cot_part, offset, row_block, 0)
            query_index = row_zero + offset + jnp.arange(row_block, dtype=jnp.int32)
            allowed = jnp.where(
                key_index[None, :] < prefix,
                key_index[None, :] < first,
                key_index[None, :] - prefix <= query_index[:, None],
            )
            scores = (
                jnp.einsum("rhd,kd->hrk", query_rows, key_one, preferred_element_type=jnp.float32)
                * scale
            )
            scores = jnp.where(allowed[None], scores, -1e30)
            highest = jnp.max(scores, axis=-1, keepdims=True)
            expo = jnp.exp(scores - highest)
            probs = expo / jnp.sum(expo, axis=-1, keepdims=True)
            probs_b = probs.astype(jnp.bfloat16)
            output = jnp.einsum(
                "hrk,kd->rhd", probs_b, value_one, preferred_element_type=jnp.float32
            ).astype(jnp.bfloat16)
            delta = jnp.sum(cot_rows.astype(jnp.float32) * output.astype(jnp.float32), axis=-1).T
            dprobs = jnp.einsum(
                "rhd,kd->hrk", cot_rows, value_one, preferred_element_type=jnp.float32
            )
            dscore = (probs * (dprobs - delta[:, :, None])).astype(jnp.bfloat16)
            grad_query = (
                jnp.einsum("hrk,kd->rhd", dscore, key_one, preferred_element_type=jnp.float32)
                * scale
            ).astype(jnp.bfloat16)
            grad_key = (
                grad_key
                + jnp.einsum(
                    "hrk,rhd->kd",
                    dscore[:, :, prefix:],
                    query_rows,
                    preferred_element_type=jnp.float32,
                )
                * scale
            )
            grad_value = grad_value + jnp.einsum(
                "hrk,rhd->kd", probs_b[:, :, prefix:], cot_rows, preferred_element_type=jnp.float32
            )
            return ((grad_key, grad_value), (output, grad_query))

        empty = jnp.zeros((slab, width), jnp.float32)
        (grad_key, grad_value), (outputs, grads) = lax.scan(
            row_step, (empty, empty), jnp.arange(rows // row_block, dtype=jnp.int32)
        )
        outputs = outputs.reshape(rows, head_block, width)
        grads = grads.reshape(rows, head_block, width)
        old_key = lax.dynamic_index_in_dim(key_acc, owner, 1, keepdims=False)
        old_value = lax.dynamic_index_in_dim(value_acc, owner, 1, keepdims=False)
        key_acc = lax.dynamic_update_index_in_dim(key_acc, old_key + grad_key, owner, 1)
        value_acc = lax.dynamic_update_index_in_dim(value_acc, old_value + grad_value, owner, 1)
        return ((key_acc, value_acc), (outputs, grads))

    zeros_kv = jnp.zeros((slab, keys.shape[1], width), jnp.float32)
    (key_acc, value_acc), (outputs, grads) = lax.scan(
        head_step, (zeros_kv, zeros_kv), jnp.arange(heads // head_block, dtype=jnp.int32)
    )
    outputs = jnp.transpose(outputs, (1, 0, 2, 3)).reshape(rows, heads, width)
    grads = jnp.transpose(grads, (1, 0, 2, 3)).reshape(rows, heads, width)
    return (outputs, grads, key_acc, value_acc)


def body(q_proj, k_proj, v_proj, cache_k, cache_v, bias_q, bias_k, bias_v, start, dout):
    devices = lax.axis_size("seq")
    rank = lax.axis_index("seq")
    tokens = q_proj.shape[1]
    first = start[0]
    positions = first + rank * tokens + jnp.arange(tokens, dtype=jnp.int32)
    queries = rotary(
        (q_proj[0].astype(jnp.float32) + bias_q.astype(jnp.float32)).reshape(tokens, HQ, HD),
        positions,
    ).astype(jnp.bfloat16)
    keys = rotary(
        (k_proj[0].astype(jnp.float32) + bias_k.astype(jnp.float32)).reshape(tokens, KV, HD),
        positions,
    ).astype(jnp.bfloat16)
    values = (
        (v_proj[0].astype(jnp.float32) + bias_v.astype(jnp.float32))
        .astype(jnp.bfloat16)
        .reshape(tokens, KV, HD)
    )
    cotangent = dout[0].reshape(tokens, HQ, HD)
    cached_keys = cache_k[0].reshape(cache_k.shape[1], KV, HD)
    cached_values = cache_v[0].reshape(cache_v.shape[1], KV, HD)
    copies = max(devices // KV, 1)
    keys_wide = jnp.repeat(keys, copies, axis=1)
    values_wide = jnp.repeat(values, copies, axis=1)
    cache_keys_wide = jnp.repeat(cached_keys, copies, axis=1)
    cache_values_wide = jnp.repeat(cached_values, copies, axis=1)
    head_queries, head_keys, head_values, head_cot = (
        lax.all_to_all(queries, "seq", split_axis=1, concat_axis=0, tiled=True),
        lax.all_to_all(keys_wide, "seq", split_axis=1, concat_axis=0, tiled=True),
        lax.all_to_all(values_wide, "seq", split_axis=1, concat_axis=0, tiled=True),
        lax.all_to_all(cotangent, "seq", split_axis=1, concat_axis=0, tiled=True),
    )
    head_cache_keys, head_cache_values = (
        lax.all_to_all(cache_keys_wide, "seq", split_axis=1, concat_axis=0, tiled=True),
        lax.all_to_all(cache_values_wide, "seq", split_axis=1, concat_axis=0, tiled=True),
    )
    prefix = head_cache_keys.shape[0]
    all_keys = jnp.concatenate([head_cache_keys, head_keys], axis=0)
    all_values = jnp.concatenate([head_cache_values, head_values], axis=0)
    outputs, dq_rot, dk_rot, dv_all = attend(
        head_queries, head_cot, all_keys, all_values, first, 0, prefix
    )
    out_tokens, dq_tokens = (
        lax.all_to_all(outputs, "seq", split_axis=0, concat_axis=1, tiled=True),
        lax.all_to_all(dq_rot, "seq", split_axis=0, concat_axis=1, tiled=True),
    )
    dk_copies, dv_copies = (
        lax.all_to_all(
            dk_rot.astype(jnp.bfloat16), "seq", split_axis=0, concat_axis=1, tiled=True
        ).astype(dk_rot.dtype),
        lax.all_to_all(
            dv_all.astype(jnp.bfloat16), "seq", split_axis=0, concat_axis=1, tiled=True
        ).astype(dv_all.dtype),
    )
    dk_tokens = jnp.sum(dk_copies.reshape(tokens, KV, copies, HD), axis=2)
    dv_tokens = jnp.sum(dv_copies.reshape(tokens, KV, copies, HD), axis=2)
    grad_query = rotary_back(dq_tokens.astype(jnp.float32), positions)
    grad_key = rotary_back(dk_tokens, positions)
    sums_query, sums_key, sums_value = lax.psum(
        (
            jnp.sum(grad_query, axis=0).reshape(HQ * HD),
            jnp.sum(grad_key, axis=0).reshape(KV * HD),
            jnp.sum(dv_tokens, axis=0).reshape(KV * HD),
        ),
        ("dp", "seq"),
    )
    return (
        out_tokens.reshape(1, tokens, HQ * HD),
        grad_query.astype(jnp.bfloat16).reshape(1, tokens, HQ * HD),
        grad_key.astype(jnp.bfloat16).reshape(1, tokens, KV * HD),
        dv_tokens.astype(jnp.bfloat16).reshape(1, tokens, KV * HD),
        sums_query,
        sums_key,
        sums_value,
    )


def solution(mesh):
    placed = (
        P("dp", "seq", None),
        P("dp", "seq", None),
        P("dp", "seq", None),
        P("dp", "seq", None),
        P("dp", "seq", None),
        P(),
        P(),
        P(),
        P("dp"),
        P("dp", "seq", None),
    )
    return jax.shard_map(
        body,
        mesh=mesh,
        in_specs=placed,
        out_specs=(
            P("dp", "seq", None),
            P("dp", "seq", None),
            P("dp", "seq", None),
            P("dp", "seq", None),
            P(),
            P(),
            P(),
        ),
        check_vma=False,
    )
```

profile of v0, /device:TPU:1, one launch (start us, length us, event | category | flops | bytes accessed | tf_op | source)
XLA Modules:
  0.0 376.5 jit_solution(17324488417311112449)
XLA Ops:
  2.4 6.5 %all-to-all-start.2 = ((bf16[128,8,128]{2,0,1:T(8,128)(2,1)}), bf16[128,8,128]{2,0,1:T(8,128)(2,1)S(1)}, u32[]{:S(2)}, u32[]{:S(2)}) async-start(bf16[128,8,128]{2,0,1:T(8,128)(2,1)} %bitcast.11), calls=%async_computation.2 | async-start | bytes 524288 | tf_op jit(solution)/shard_map/all_to_all | solution.py:158
  15.8 3.4 all-to-all-start.4
  19.3 6.0 %all-to-all-done.4 = bf16[128,8,128]{2,0,1:T(8,128)(2,1)S(1)} async-done(((bf16[128,8,128]{2,0,1:T(8,128)(2,1)}), bf16[128,8,128]{2,0,1:T(8,128)(2,1)S(1)}, u32[]{:S(2)}, u32[]{:S(2)}) %all-to-all-start.4) | async-done | bytes 262176 | tf_op jit(solution)/shard_map/all_to_all | solution.py:159
  26.1 3.4 all-to-all-start.5
  29.8 5.8 %all-to-all-done.5 = bf16[128,8,128]{2,0,1:T(8,128)(2,1)S(1)} async-done(((bf16[128,8,128]{2,0,1:T(8,128)(2,1)}), bf16[128,8,128]{2,0,1:T(8,128)(2,1)S(1)}, u32[]{:S(2)}, u32[]{:S(2)}) %all-to-all-start.5) | async-done | bytes 262176 | tf_op jit(solution)/shard_map/all_to_all | solution.py:154
  36.4 3.4 all-to-all-start.3
  41.2 4.7 %all-to-all-done.3 = bf16[128,8,128]{2,0,1:T(8,128)(2,1)S(1)} async-done(((bf16[128,8,128]{2,0,1:T(8,128)(2,1)}), bf16[128,8,128]{2,0,1:T(8,128)(2,1)S(1)}, u32[]{:S(2)}, u32[]{:S(2)}) %all-to-all-start.3) | async-done | bytes 262176 | tf_op jit(solution)/shard_map/all_to_all | solution.py:153
  45.9 3.7 all-to-all-start.1
  53.5 6.5 %all-to-all-done.1 = bf16[128,32,128]{0,2,1:T(8,128)(2,1)S(1)} async-done(((bf16[128,32,128]{0,2,1:T(8,128)(2,1)}), bf16[128,32,128]{0,2,1:T(8,128)(2,1)S(1)}, u32[]{:S(2)}, u32[]{:S(2)}) %all-to-all-start.1) | async-done | bytes 1048608 | tf_op jit(solution)/shard_map/all_to_all | solution.py:155
  60.0 3.6 all-to-all-start
  66.7 7.2 %all-to-all-done = bf16[128,32,128]{2,0,1:T(8,128)(2,1)S(1)} async-done(((bf16[128,32,128]{2,0,1:T(8,128)(2,1)}), bf16[128,32,128]{2,0,1:T(8,128)(2,1)S(1)}, u32[]{:S(2)}, u32[]{:S(2)}) %all-to-all-start) | async-done | bytes 1048608 | tf_op jit(solution)/shard_map/all_to_all | solution.py:152
  75.0 139.6 %while.59 = (s32[]{:T(128)}, f32[1024,1,128]{2,0,1:T(8,128)S(1)}, f32[1024,1,128]{2,0,1:T(8,128)S(1)}, bf16[4,1024,1,128]{3,1,2,0:T(8,128)(2,1)}, bf16[4,1024,1,...) while((s32[]{:T(128)}, f32[1024,1,128]{2,0,1:T(8,128)S(1)}, ...), condition=%wide.region_6.7_spmd.clone.clone, body=%wide.region_0.6_spmd.clone.clone.sunk | while | flops 1359287296 | bytes 49224388 | solution.py:116
  79.6 28.5 %while.60 = (s32[]{:T(128)}, f32[1024,128]{1,0:T(8,128)S(1)}, f32[1024,128]{1,0:T(8,128)S(1)}, bf16[2,512,1,128]{3,1,0,2:T(8,128)(2,1)}, bf16[2,512,1,128]{3,1,2...) while((s32[]{:T(128)}, f32[1024,128]{1,0:T(8,128)S(1)}, ...), condition=%wide.region_5.5_spmd.clone.clone, body=%wide.region_1.4_spmd.clone.clone.sunk | while | flops 1359025152 | bytes 41875732 | solution.py:104
  114.5 28.5 %while.60 = (s32[]{:T(128)}, f32[1024,128]{1,0:T(8,128)S(1)}, f32[1024,128]{1,0:T(8,128)S(1)}, bf16[2,512,1,128]{3,1,0,2:T(8,128)(2,1)}, bf16[2,512,1,128]{3,1,2...) while((s32[]{:T(128)}, f32[1024,128]{1,0:T(8,128)S(1)}, ...), condition=%wide.region_5.5_spmd.clone.clone, body=%wide.region_1.4_spmd.clone.clone.sunk | while | flops 1359025152 | bytes 41875732 | solution.py:104
  149.4 28.5 %while.60 = (s32[]{:T(128)}, f32[1024,128]{1,0:T(8,128)S(1)}, f32[1024,128]{1,0:T(8,128)S(1)}, bf16[2,512,1,128]{3,1,0,2:T(8,128)(2,1)}, bf16[2,512,1,128]{3,1,2...) while((s32[]{:T(128)}, f32[1024,128]{1,0:T(8,128)S(1)}, ...), condition=%wide.region_5.5_spmd.clone.clone, body=%wide.region_1.4_spmd.clone.clone.sunk | while | flops 1359025152 | bytes 41875732 | solution.py:104
  184.3 28.5 %while.60 = (s32[]{:T(128)}, f32[1024,128]{1,0:T(8,128)S(1)}, f32[1024,128]{1,0:T(8,128)S(1)}, bf16[2,512,1,128]{3,1,0,2:T(8,128)(2,1)}, bf16[2,512,1,128]{3,1,2...) while((s32[]{:T(128)}, f32[1024,128]{1,0:T(8,128)S(1)}, ...), condition=%wide.region_5.5_spmd.clone.clone, body=%wide.region_1.4_spmd.clone.clone.sunk | while | flops 1359025152 | bytes 41875732 | solution.py:104
  216.8 3.4 all-to-all-start.8
  221.8 4.5 %all-to-all-done.8 = bf16[8,2,8192]{2,1,0:T(2,128)(2,1)S(1)} async-done(((bf16[8,2,8192]{2,1,0:T(2,128)(2,1)}), bf16[8,2,8192]{2,1,0:T(2,128)(2,1)S(1)}, u32[]{:S(2)}, u32[]{:S(2)}) %all-to-all-start.8) | async-done | bytes 262176 | tf_op jit(solution)/shard_map/all_to_all | solution.py:172
  226.3 3.6 all-to-all-start.9
  233.0 3.2 all-to-all-done.9
  236.2 3.6 all-to-all-start.6
  241.6 9.9 %all-to-all-done.6 = bf16[1024,4,128]{2,1,0:T(4,128)(2,1)S(1)} async-done(((bf16[1024,4,128]{2,1,0:T(4,128)(2,1)}), bf16[1024,4,128]{2,1,0:T(4,128)(2,1)S(1)}, u32[]{:S(2)}, u32[]{:S(2)}) %all-to-all-start.6) | async-done | bytes 1048608 | tf_op jit(solution)/shard_map/all_to_all | solution.py:168
  251.5 3.6 all-to-all-start.7
  286.0 90.5 %all-reduce = (f32[4096]{0:T(1024)}, f32[512]{0:T(512)}, f32[512]{0:T(512)}) all-reduce(f32[4096]{0:T(1024)S(1)} %bitcast.274, f32[512]{0:T(512)S(1)} %bitcast.276, f32[512]{0:T(512)S(1)} %bitcast.277), channel_id=1, replica_groups=mesh['dp'=32,'seq'=8] {'dp','seq'}, use_global_device_ids=true, to_apply=%region_10.11 | all-reduce | flops 5120 | bytes 40960 | tf_op jit(solution)/shard_map/psum | solution.py:183
  (330 shorter events, 184.0 us)
Async XLA Ops:
  0.6 10.7 %copy-start.22 = (bf16[1,128,512]{2,1,0:T(8,128)(2,1)S(1)}, bf16[1,128,512]{2,1,0:T(8,128)(2,1)}, u32[]{:S(2)}) copy-start(bf16[1,128,512]{2,1,0:T(8,128)(2,1)} %param.15) | copy-start | bytes 393220
  0.6 10.9 %copy-start.23 = (bf16[1,128,512]{2,1,0:T(8,128)(2,1)S(1)}, bf16[1,128,512]{2,1,0:T(8,128)(2,1)}, u32[]{:S(2)}) copy-start(bf16[1,128,512]{2,1,0:T(8,128)(2,1)} %param.18) | copy-start | bytes 393220
  2.4 16.9 %copy-start.25 = (bf16[512]{0:T(512)(128)(2,1)S(1)}, bf16[512]{0:T(512)(128)(2,1)}, u32[]{:S(2)}) copy-start(bf16[512]{0:T(512)(128)(2,1)} %param.20) | copy-start | bytes 3076
  2.4 12.7 %all-to-all-start.2 = ((bf16[128,8,128]{2,0,1:T(8,128)(2,1)}), bf16[128,8,128]{2,0,1:T(8,128)(2,1)S(1)}, u32[]{:S(2)}, u32[]{:S(2)}) async-start(bf16[128,8,128]{2,0,1:T(8,128)(2,1)} %bitcast.11), calls=%async_computation.2 | async-start | bytes 524288 | tf_op jit(solution)/shard_map/all_to_all | solution.py:158
  12.1 37.5 %copy-start.8 = (f32[128,128]{1,0:T(8,128)}, f32[128,128]{1,0:T(8,128)S(1)}, u32[]{:S(2)}) copy-start(f32[128,128]{1,0:T(8,128)S(1)} %get-tuple-element.735) | copy-start | bytes 196612
  12.1 37.6 %copy-start.6 = (f32[128,128]{1,0:T(8,128)}, f32[128,128]{1,0:T(8,128)S(1)}, u32[]{:S(2)}) copy-start(f32[128,128]{1,0:T(8,128)S(1)} %get-tuple-element.734) | copy-start | bytes 196612
  15.8 9.5 %all-to-all-start.4 = ((bf16[128,8,128]{2,0,1:T(8,128)(2,1)}), bf16[128,8,128]{2,0,1:T(8,128)(2,1)S(1)}, u32[]{:S(2)}, u32[]{:S(2)}) async-start(bf16[128,8,128]{2,0,1:T(8,128)(2,1)} %bitcast.21), calls=%async_computation.4 | async-start | bytes 524288 | tf_op jit(solution)/shard_map/all_to_all | solution.py:159
  19.3 20.5 %copy-start.10 = (bf16[1,128,4096]{2,1,0:T(8,128)(2,1)S(1)}, bf16[1,128,4096]{2,1,0:T(8,128)(2,1)}, u32[]{:S(2)}) copy-start(bf16[1,128,4096]{2,1,0:T(8,128)(2,1)} %param.23) | copy-start | bytes 3145732
  25.3 15.8 %copy-start.13 = (bf16[128,8,128]{2,0,1:T(8,128)(2,1)}, bf16[128,8,128]{2,0,1:T(8,128)(2,1)S(1)}, u32[]{:S(2)}) copy-start(bf16[128,8,128]{2,0,1:T(8,128)(2,1)S(1)} %all-to-all-done.4) | copy-start | bytes 786436
  26.1 9.5 %all-to-all-start.5 = ((bf16[128,8,128]{2,0,1:T(8,128)(2,1)}), bf16[128,8,128]{2,0,1:T(8,128)(2,1)S(1)}, u32[]{:S(2)}, u32[]{:S(2)}) async-start(bf16[128,8,128]{2,0,1:T(8,128)(2,1)} %bitcast.26), calls=%async_computation.5 | async-start | bytes 524288 | tf_op jit(solution)/shard_map/all_to_all | solution.py:154
  36.4 9.5 %all-to-all-start.3 = ((bf16[128,8,128]{2,0,1:T(8,128)(2,1)}), bf16[128,8,128]{2,0,1:T(8,128)(2,1)S(1)}, u32[]{:S(2)}, u32[]{:S(2)}) async-start(bf16[128,8,128]{2,0,1:T(8,128)(2,1)} %bitcast.17), calls=%async_computation.3 | async-start | bytes 524288 | tf_op jit(solution)/shard_map/all_to_all | solution.py:153
  39.8 10.0 %copy-start.11 = (bf16[1,128,4096]{2,1,0:T(8,128)(2,1)S(1)}, bf16[1,128,4096]{2,1,0:T(8,128)(2,1)}, u32[]{:S(2)}) copy-start(bf16[1,128,4096]{2,1,0:T(8,128)(2,1)} %param.14) | copy-start | bytes 3145732
  45.9 3.8 %copy-start.17 = (bf16[128,8,128]{2,0,1:T(8,128)(2,1)}, bf16[128,8,128]{2,0,1:T(8,128)(2,1)S(1)}, u32[]{:S(2)}) copy-start(bf16[128,8,128]{2,0,1:T(8,128)(2,1)S(1)} %all-to-all-done.3) | copy-start | bytes 786436
  45.9 4.6 %copy-start.24 = (bf16[4096]{0:T(1024)(128)(2,1)S(1)}, bf16[4096]{0:T(1024)(128)(2,1)}, u32[]{:S(2)}) copy-start(bf16[4096]{0:T(1024)(128)(2,1)} %param.19) | copy-start | bytes 24580
  45.9 14.1 %all-to-all-start.1 = ((bf16[128,32,128]{0,2,1:T(8,128)(2,1)}), bf16[128,32,128]{0,2,1:T(8,128)(2,1)S(1)}, u32[]{:S(2)}, u32[]{:S(2)}) async-start(bf16[128,32,128]{0,2,1:T(8,128)(2,1)} %bitcast.6), calls=%async_computation.1 | async-start | bytes 2097152 | tf_op jit(solution)/shard_map/all_to_all | solution.py:155
  52.2 11.4 %copy-start.14 = (bf16[128,8,128]{2,0,1:T(8,128)(2,1)S(1)}, bf16[128,8,128]{2,0,1:T(8,128)(2,1)}, u32[]{:S(2)}) copy-start(bf16[128,8,128]{2,0,1:T(8,128)(2,1)} %copy-done.13) | copy-start | bytes 786436
  52.2 11.4 %copy-start.16 = (bf16[128,8,128]{2,0,1:T(8,128)(2,1)S(1)}, bf16[128,8,128]{2,0,1:T(8,128)(2,1)}, u32[]{:S(2)}) copy-start(bf16[128,8,128]{2,0,1:T(8,128)(2,1)} %copy-done.15) | copy-start | bytes 786436
  60.0 13.9 %all-to-all-start = ((bf16[128,32,128]{2,0,1:T(8,128)(2,1)}), bf16[128,32,128]{2,0,1:T(8,128)(2,1)S(1)}, u32[]{:S(2)}, u32[]{:S(2)}) async-start(bf16[128,32,128]{2,0,1:T(8,128)(2,1)} %copy.142), calls=%async_computation | async-start | bytes 2097152 | tf_op jit(solution)/shard_map/all_to_all | solution.py:152
  216.8 9.5 %all-to-all-start.8 = ((bf16[8,2,8192]{2,1,0:T(2,128)(2,1)}), bf16[8,2,8192]{2,1,0:T(2,128)(2,1)S(1)}, u32[]{:S(2)}, u32[]{:S(2)}) async-start(bf16[8,2,8192]{2,1,0:T(2,128)(2,1)} %reshape.436), calls=%async_computation.8 | async-start | bytes 524288 | tf_op jit(solution)/shard_map/all_to_all | solution.py:172
  226.3 10.0 %all-to-all-start.9 = ((bf16[8,2,8192]{2,1,0:T(2,128)(2,1)}), bf16[8,2,8192]{2,1,0:T(2,128)(2,1)S(1)}, u32[]{:S(2)}, u32[]{:S(2)}) async-start(bf16[8,2,8192]{2,1,0:T(2,128)(2,1)} %reshape.438), calls=%async_computation.9 | async-start | bytes 524288 | tf_op jit(solution)/shard_map/all_to_all | solution.py:175
  229.9 9.9 %copy-start.12 = (bf16[4,1024,1,128]{3,1,2,0:T(8,128)(2,1)S(1)}, bf16[4,1024,1,128]{3,1,2,0:T(8,128)(2,1)}, u32[]{:S(2)}) copy-start(bf16[4,1024,1,128]{3,1,2,0:T(8,128)(2,1)} %get-tuple-element.348) | copy-start | bytes 3145732
  236.2 15.3 %all-to-all-start.6 = ((bf16[1024,4,128]{2,1,0:T(4,128)(2,1)}), bf16[1024,4,128]{2,1,0:T(4,128)(2,1)S(1)}, u32[]{:S(2)}, u32[]{:S(2)}) async-start(bf16[1024,4,128]{2,1,0:T(4,128)(2,1)} %copy.153), calls=%async_computation.6 | async-start | bytes 2097152 | tf_op jit(solution)/shard_map/all_to_all | solution.py:168
  251.5 16.6 %all-to-all-start.7 = ((bf16[1024,4,128]{2,1,0:T(4,128)(2,1)}), bf16[1024,4,128]{2,1,0:T(4,128)(2,1)S(1)}, u32[]{:S(2)}, u32[]{:S(2)}) async-start(bf16[1024,4,128]{2,1,0:T(4,128)(2,1)} %bitcast.260), calls=%async_computation.7 | async-start | bytes 2097152 | tf_op jit(solution)/shard_map/all_to_all | solution.py:169
  255.4 5.0 %copy-start.9 = (f32[128,128]{1,0:T(8,128)S(1)}, f32[128,128]{1,0:T(8,128)}, u32[]{:S(2)}) copy-start(f32[128,128]{1,0:T(8,128)} %copy-done.8) | copy-start | bytes 196612
  (25 other events, 60.5 us)
where the time goes:
time: 379 us; the launch traced here: 376 us
  blocking collectives  90.5 us (24%)
  matrix products  79 us (21%)
  local copies, waits for them, and re-layouts  62 us (16%)
  waiting for transfers between devices  53.1 us (14%)
  starting transfers between devices  38.1 us (10%)
  other arithmetic  37.6 us (10%)
  loops' own time  14.1 us (4%)
    psum x1, blocking collectives, body(): lax.psum((jnp.sum(grad_query, axis=0).reshape(HQ * HD), jnp.sum(grad_key,...  90.5 us
    dot_general x8, matrix products, row_step(): jnp.einsum('hrk,kd->rhd', dscore, key_one, preferred_element_type=jnp.flo...  24.6 us
    dot_general x8, matrix products, row_step(): jnp.einsum('rhd,kd->hrk', cot_rows, value_one, preferred_element_type=jnp...  19.4 us
    dot_general x8, matrix products, row_step(): jnp.einsum('rhd,kd->hrk', query_rows, key_one, preferred_element_type=jnp...  18.6 us
    all_to_all x1, waiting for transfers between devices, body(): lax.all_to_all(outputs, 'seq', split_axis=0, concat_axis=1, tiled=True)  9.94 us
    another operation x1, loops' own time, attend(): lax.scan(head_step, (zeros_kv, zeros_kv), jnp.arange(heads // head_block,...  8.13 us
    unnamed x57, local copies, waits for them, and re-layouts  7.6 us
  transfers between devices with their start and end apart: 10, of which 10 were waited for; matrix products, arithmetic and copies ran while one was open for 7% of the time, Pallas kernels for 0%

commit v1 on v0

v1 whole, which is shorter than its diff:
```python
import functools

import jax
import jax.numpy as jnp
import numpy as np
from jax import lax
from jax.experimental import pallas as pl
from jax.experimental.pallas import tpu as pltpu
from jax.sharding import PartitionSpec as P

HQ = 32
KV = 4
HD = 128
GROUP = 8
SCALE = float(HD**-0.5)
EXP2_SCALE = float(np.log2(np.e) * HD**-0.5)
f32 = jnp.float32
bf16 = jnp.bfloat16


def rotary_tables(positions):
    half = HD // 2
    freqs = jnp.exp(
        -(2.0 * jnp.arange(half, dtype=f32) / HD) * jnp.log(jnp.float32(1000000.0))
    )
    angles = positions.astype(f32)[:, None] * freqs[None, :]
    cosine, sine = jnp.cos(angles), jnp.sin(angles)
    return (
        jnp.concatenate([cosine, cosine], axis=1),
        jnp.concatenate([-sine, sine], axis=1),
    )


def dot(a, b, contract_a, contract_b):
    return lax.dot_general(
        a, b, (((contract_a,), (contract_b,)), ((), ())), preferred_element_type=f32
    )


def turn(x):
    return pltpu.roll(x, HD // 2, axis=1)


def attend_kernel(
    n,
    start_ref, q_ref, k_ref, v_ref, ck_ref, cv_ref, bq_ref, bk_ref, bv_ref, cos_ref, sin_ref, do_ref,
    out_ref, gq_ref, gk_ref, gv_ref, sums_ref,
    kv, rsend, rrecv, q_s, do_s, s_ref, p_ref, mask_ref, stat, norm, acc, q_t, do_t, do_n,
    kv_send, kv_recv, r_send, r_recv,
):
    me = lax.axis_index("seq")
    tokens = q_ref.shape[0]
    keys = n * tokens
    rows = GROUP * tokens

    barrier = pltpu.get_barrier_semaphore()

    def greet(i, _):
        pl.semaphore_signal(barrier, inc=1, device_id={"seq": lax.rem(me + i, n)}, device_id_type=pl.DeviceIdType.MESH)
        return 0

    lax.fori_loop(1, n, greet, 0)

    cosine, sine = cos_ref[...], sin_ref[...]
    for h in range(KV):
        cols = slice(h * HD, (h + 1) * HD)
        x = k_ref[:, cols].astype(f32) + bk_ref[:, cols].astype(f32)
        kv[h, 0, 1, me] = (x * cosine + turn(x) * sine).astype(bf16)
        kv[h, 1, 1, me] = (v_ref[:, cols].astype(f32) + bv_ref[:, cols].astype(f32)).astype(bf16)
        kv[h, 0, 0, me] = ck_ref[:, cols]
        kv[h, 1, 0, me] = cv_ref[:, cols]

    pl.semaphore_wait(barrier, n - 1)

    def kv_copy(h, owner, peer):
        block = kv.at[h, :, :, owner]
        return pltpu.make_async_remote_copy(
            src_ref=block, dst_ref=block, send_sem=kv_send.at[h, peer], recv_sem=kv_recv.at[h, owner],
            device_id={"seq": peer}, device_id_type=pl.DeviceIdType.MESH,
        )

    def r_copy(h, source, peer):
        return pltpu.make_async_remote_copy(
            src_ref=rsend.at[h, :, peer], dst_ref=rrecv.at[h, :, source],
            send_sem=r_send.at[h, peer], recv_sem=r_recv.at[h, source],
            device_id={"seq": peer}, device_id_type=pl.DeviceIdType.MESH,
        )

    def send_head(h, _):
        def send(i, _):
            kv_copy(h, me, lax.rem(me + i, n)).start()
            return 0

        return lax.fori_loop(1, n, send, 0)

    lax.fori_loop(0, KV, send_head, 0)

    row = lax.broadcasted_iota(jnp.int32, (tokens, keys), 0)
    col = lax.broadcasted_iota(jnp.int32, (tokens, keys), 1)
    mask_ref[0] = jnp.where(col < start_ref[0], 0.0, -1e30)
    mask_ref[1] = jnp.where(col <= row + me * tokens, 0.0, -1e30)

    def load_queries(h, _):
        for g in range(GROUP):
            cols = pl.ds(pl.multiple_of((h * GROUP + g) * HD, HD), HD)
            x = q_ref[:, cols].astype(f32) + bq_ref[:, cols].astype(f32)
            q_s[h, g * tokens : (g + 1) * tokens, :] = (x * cosine + turn(x) * sine).astype(bf16)
            do_s[h, g * tokens : (g + 1) * tokens, :] = do_ref[:, cols]
        return 0

    lax.fori_loop(0, KV, load_queries, 0)

    def head(h, _):
        def await_keys(i, _):
            source = lax.rem(me + i, n)
            kv_copy(h, source, source).wait_recv()
            return 0

        lax.fori_loop(1, n, await_keys, 0)

        q_t[...] = q_s[h].T
        stat[...] = jnp.full(stat.shape, -3e38, f32)

        def score(part, _):
            s = dot(q_s[h], kv[h, 0, part].reshape(keys, HD), 1, 1)
            s = (s.reshape(GROUP, tokens, keys) + mask_ref[part][None]).reshape(rows, keys)
            s_ref[part] = s
            m = stat[...]
            for t in range(keys // HD):
                m = jnp.maximum(m, s[:, t * HD : (t + 1) * HD])
            stat[...] = m
            return 0

        lax.fori_loop(0, 2, score, 0)
        stat[...] = jnp.broadcast_to(jnp.max(stat[...], axis=1, keepdims=True), stat.shape)
        norm[...] = jnp.zeros(norm.shape, f32)
        acc[...] = jnp.zeros(acc.shape, f32)

        def weigh(part, _):
            m = stat[...]
            pieces = [
                jnp.exp2((s_ref[part, :, t * HD : (t + 1) * HD] - m) * EXP2_SCALE)
                for t in range(keys // HD)
            ]
            norm[...] += functools.reduce(lambda a, b: a + b, pieces)
            p = jnp.concatenate([x.astype(bf16) for x in pieces], axis=1)
            p_ref[part] = p
            acc[...] += dot(p, kv[h, 1, part].reshape(keys, HD), 1, 0)
            return 0

        lax.fori_loop(0, 2, weigh, 0)
        inverse = 1.0 / jnp.sum(norm[...], axis=1, keepdims=True)
        out = (acc[...] * inverse).astype(bf16)
        for g in range(GROUP):
            cols = pl.ds(pl.multiple_of((h * GROUP + g) * HD, HD), HD)
            out_ref[:, cols] = out[g * tokens : (g + 1) * tokens]
        scaled = (do_s[h].astype(f32) * inverse).astype(bf16)
        do_n[...] = scaled
        do_t[...] = scaled.T
        delta = jnp.sum(scaled.astype(f32) * out.astype(f32), axis=1, keepdims=True)
        stat[...] = jnp.broadcast_to(delta, stat.shape)
        acc[...] = jnp.zeros(acc.shape, f32)

        def score_grad(part):
            dp = dot(do_n[...], kv[h, 1, part].reshape(keys, HD), 1, 1)
            delta = stat[...]
            ds = jnp.concatenate(
                [
                    (
                        (dp[:, t * HD : (t + 1) * HD] - delta)
                        * p_ref[part, :, t * HD : (t + 1) * HD].astype(f32)
                    ).astype(bf16)
                    for t in range(keys // HD)
                ],
                axis=1,
            )
            acc[...] += dot(ds, kv[h, 0, part].reshape(keys, HD), 1, 0)
            return ds

        ds = score_grad(1)
        rsend[h, 0] = (dot(q_t[...], ds, 1, 0).T * SCALE).astype(bf16).reshape(n, tokens, HD)
        rsend[h, 1] = dot(do_t[...], p_ref[1], 1, 0).T.astype(bf16).reshape(n, tokens, HD)

        def send_back(peer, _):
            r_copy(h, me, peer).start()
            return 0

        lax.fori_loop(0, me, send_back, 0)
        score_grad(0)
        dq = (acc[...] * SCALE).astype(bf16).astype(f32)
        for g in range(GROUP):
            cols = pl.ds(pl.multiple_of((h * GROUP + g) * HD, HD), HD)
            x = dq[g * tokens : (g + 1) * tokens]
            gq = x * cosine - turn(x) * sine
            gq_ref[:, cols] = gq.astype(bf16)
            sums_ref[h, g : g + 1, :] = jnp.sum(gq, axis=0, keepdims=True)
        return 0

    lax.fori_loop(0, KV, head, 0)

    sums_ref[KV] = jnp.zeros((GROUP, HD), f32)
    for h in range(KV):
        cols = slice(h * HD, (h + 1) * HD)

        def gather(source, total):
            r_copy(h, source, source).wait_recv()
            return total + rrecv[h, :, source].astype(f32)

        total = lax.fori_loop(me + 1, n, gather, rsend[h, :, me].astype(f32))
        gk = total[0] * cosine - turn(total[0]) * sine
        gk_ref[:, cols] = gk.astype(bf16)
        gv_ref[:, cols] = total[1].astype(bf16)
        sums_ref[KV, h : h + 1, :] = jnp.sum(gk, axis=0, keepdims=True)
        sums_ref[KV, KV + h : KV + h + 1, :] = jnp.sum(total[1], axis=0, keepdims=True)

    def drain_head(h, _):
        def drain_kv(i, _):
            kv_copy(h, me, lax.rem(me + i, n)).wait_send()
            return 0

        def drain_r(peer, _):
            r_copy(h, me, peer).wait_send()
            return 0

        lax.fori_loop(1, n, drain_kv, 0)
        return lax.fori_loop(0, me, drain_r, 0)

    lax.fori_loop(0, KV, drain_head, 0)


def sum_kernel(n, m, x_ref, out_ref, first, second, s1, r1, s2, r2, s3, r3):
    me, mine = lax.axis_index("seq"), lax.axis_index("dp")
    barrier = pltpu.get_barrier_semaphore()

    def greet(axis, size, index):
        def one(i, _):
            pl.semaphore_signal(barrier, inc=1, device_id={axis: lax.rem(index + i, size)}, device_id_type=pl.DeviceIdType.MESH)
            return 0

        lax.fori_loop(1, size, one, 0)

    greet("seq", n, me)
    greet("dp", m, mine)
    pl.semaphore_wait(barrier, n + m - 2)

    def exchange(axis, size, index, source, target, send, recv):
        def copy(owner, peer):
            return pltpu.make_async_remote_copy(
                src_ref=source(peer), dst_ref=target(owner), send_sem=send.at[peer], recv_sem=recv.at[owner],
                device_id={axis: peer}, device_id_type=pl.DeviceIdType.MESH,
            )

        def begin(i, _):
            copy(index, lax.rem(index + i, size)).start()
            return 0

        def arrive(i, _):
            peer = lax.rem(index + i, size)
            copy(peer, peer).wait_recv()
            return 0

        def leave(i, _):
            copy(index, lax.rem(index + i, size)).wait_send()
            return 0

        lax.fori_loop(1, size, begin, 0)
        lax.fori_loop(1, size, arrive, 0)
        return lambda: lax.fori_loop(1, size, leave, 0)

    first[me] = x_ref[me]
    leave_first = exchange("seq", n, me, lambda peer: x_ref.at[peer], lambda owner: first.at[owner], s1, r1)
    second[mine] = jnp.sum(first[...], axis=0)
    leave_second = exchange("dp", m, mine, lambda peer: second.at[mine], lambda owner: second.at[owner], s2, r2)
    out_ref[me] = jnp.sum(second[...], axis=0)
    leave_third = exchange("seq", n, me, lambda peer: out_ref.at[me], lambda owner: out_ref.at[owner], s3, r3)
    leave_first()
    leave_second()
    leave_third()


def body(n, m, q_proj, k_proj, v_proj, cache_k, cache_v, bias_q, bias_k, bias_v, start, dout):
    rank = lax.axis_index("seq")
    tokens = q_proj.shape[1]
    keys, rows = n * tokens, GROUP * tokens
    cosine, sine = rotary_tables(start[0] + rank * tokens + jnp.arange(tokens, dtype=jnp.int32))
    vmem = pl.BlockSpec(memory_space=pltpu.VMEM)
    dma = pltpu.SemaphoreType.DMA
    out, grad_q, grad_k, grad_v, sums = pl.pallas_call(
        functools.partial(attend_kernel, n),
        out_shape=[
            jax.ShapeDtypeStruct((tokens, HQ * HD), bf16),
            jax.ShapeDtypeStruct((tokens, HQ * HD), bf16),
            jax.ShapeDtypeStruct((tokens, KV * HD), bf16),
            jax.ShapeDtypeStruct((tokens, KV * HD), bf16),
            jax.ShapeDtypeStruct((KV + 1, GROUP, HD), f32),
        ],
        in_specs=[pl.BlockSpec(memory_space=pltpu.SMEM)] + [vmem] * 11,
        out_specs=[vmem] * 5,
        scratch_shapes=[
            pltpu.VMEM((KV, 2, 2, n, tokens, HD), bf16),
            pltpu.VMEM((KV, 2, n, tokens, HD), bf16),
            pltpu.VMEM((KV, 2, n, tokens, HD), bf16),
            pltpu.VMEM((KV, rows, HD), bf16),
            pltpu.VMEM((KV, rows, HD), bf16),
            pltpu.VMEM((2, rows, keys), f32),
            pltpu.VMEM((2, rows, keys), bf16),
            pltpu.VMEM((2, tokens, keys), f32),
            pltpu.VMEM((rows, HD), f32),
            pltpu.VMEM((rows, HD), f32),
            pltpu.VMEM((rows, HD), f32),
            pltpu.VMEM((HD, rows), bf16),
            pltpu.VMEM((HD, rows), bf16),
            pltpu.VMEM((rows, HD), bf16),
            dma((KV, n)),
            dma((KV, n)),
            dma((KV, n)),
            dma((KV, n)),
        ],
        compiler_params=pltpu.CompilerParams(collective_id=0, has_side_effects=True, vmem_limit_bytes=60 << 20),
        name="attend",
    )(
        start, q_proj[0], k_proj[0], v_proj[0], cache_k[0], cache_v[0],
        bias_q[None], bias_k[None], bias_v[None], cosine, sine, dout[0],
    )
    slots = (KV + 1) * GROUP // n
    packed = jnp.pad(sums.reshape(n, slots, HD), ((0, 0), (0, 8 - slots), (0, 0)))
    total = pl.pallas_call(
        functools.partial(sum_kernel, n, m),
        out_shape=jax.ShapeDtypeStruct((n, 8, HD), f32),
        in_specs=[vmem],
        out_specs=vmem,
        scratch_shapes=[pltpu.VMEM((n, 8, HD), f32), pltpu.VMEM((m, 8, HD), f32)]
        + [dma((n,)), dma((n,)), dma((m,)), dma((m,)), dma((n,)), dma((n,))],
        compiler_params=pltpu.CompilerParams(collective_id=1, has_side_effects=True),
        name="bias_sums",
    )(packed)
    total = total[:, :slots].reshape((KV + 1) * GROUP * HD)
    split = HQ * HD
    return (
        out[None], grad_q[None], grad_k[None], grad_v[None],
        total[:split], total[split : split + KV * HD], total[split + KV * HD :],
    )


def solution(mesh):
    n, m = mesh.shape["seq"], mesh.shape["dp"]
    tokens = P("dp", "seq", None)
    return jax.shard_map(
        functools.partial(body, n, m),
        mesh=mesh,
        in_specs=(tokens, tokens, tokens, tokens, tokens, P(), P(), P(), P("dp"), tokens),
        out_specs=(tokens, tokens, tokens, tokens, P(), P(), P()),
        check_vma=False,
    )
```

time: 379 us -> 121 us (0.32)
  Pallas kernels: 0 us -> 108 us
  blocking collectives: 90.5 us -> 0 us
  matrix products: 79 us -> 0 us
  waiting for transfers between devices: 53.1 us -> 0 us
  local copies, waits for them, and re-layouts: 62 us -> 10.9 us
  starting transfers between devices: 38.1 us -> 0 us
  other arithmetic: 37.6 us -> 1.08 us
  loops' own time: 14.1 us -> 0 us
    pallas_call x0 -> x2, Pallas kernels: none -> 108 us  [the longest x1 79.3 us: body(): pl.pallas_call(functools.partial(attend_kernel, n), out_shape=[jax.ShapeD...]
    psum x1 -> x0, blocking collectives: 90.5 us -> none  [body(): lax.psum((jnp.sum(grad_query, axis=0).reshape(HQ * HD), jnp.sum(grad_key,...]
    dot_general x48 -> x0, matrix products: 79 us -> none  [the longest x8 24.6 us: row_step(): jnp.einsum('hrk,kd->rhd', dscore, key_one, preferred_element_type=jnp.flo...]
    all_to_all x10 -> x0, waiting for transfers between devices: 53.1 us -> none  [the longest x1 9.94 us: body(): lax.all_to_all(outputs, 'seq', split_axis=0, concat_axis=1, tiled=True)]
    all_to_all x10 -> x0, starting transfers between devices: 38.1 us -> none  [the longest x1 6.51 us: body(): lax.all_to_all(cache_keys_wide, 'seq', split_axis=1, concat_axis=0, tiled...]
    dynamic_slice x36 -> x0, local copies, waits for them, and re-layouts: 15.9 us -> none  [the longest x8 4.69 us: head_step(): lax.scan(row_step, (empty, empty), jnp.arange(rows // row_block, dtype=jn...]
    another operation x5 -> x0, loops' own time: 14.1 us -> none  [the longest x1 8.13 us: attend(): lax.scan(head_step, (zeros_kv, zeros_kv), jnp.arange(heads // head_block,...]
    convert_element_type x20 -> x1, other arithmetic: 11.8 us -> 0.01 us  [rotary_tables(): angles = positions.astype(f32)[:, None] * freqs[None, :]]
  transfers between devices with their start and end apart: 10 -> 0, of which waited for: 10 -> 0; matrix products, arithmetic and copies ran while one was open for 7% -> 0% of each run, Pallas kernels for 0% -> 0%
where the time goes in v1:
time: 121 us
  Pallas kernels  108 us (89%)
  local copies, waits for them, and re-layouts  10.9 us (9%)
  between operations  1.34 us (1%)
    pallas_call x1, Pallas kernels, body(): pl.pallas_call(functools.partial(attend_kernel, n), out_shape=[jax.ShapeD...  79.3 us
    pallas_call x1, Pallas kernels, body(): pl.pallas_call(functools.partial(sum_kernel, n, m), out_shape=jax.ShapeDt...  28.2 us
    unnamed x16, local copies, waits for them, and re-layouts  5.78 us

profile of v1, /device:TPU:1, one launch (start us, length us, event | category | flops | bytes accessed | tf_op | source)
XLA Modules:
  0.0 120.8 jit_solution(6712882268404050827)
XLA Ops:
  1.3 0.0 copy-start.3
  1.3 0.0 copy-start.4
  1.3 0.7 copy-done.4
  2.0 0.6 broadcast_in_dim.24.bk_ref
  2.6 0.1 copy-done.5
  2.7 0.6 broadcast_in_dim.25.bv_ref
  3.3 0.0 copy-done.3
  3.3 0.6 broadcast_in_dim.23.bq_ref
  3.9 0.3 fusion
  4.2 0.8 pad_maximum_fusion
  4.9 79.3 %attend.1 = (bf16[128,4096]{1,0:T(8,128)(2,1)}, bf16[128,4096]{1,0:T(8,128)(2,1)}, bf16[128,512]{1,0:T(8,128)(2,1)}, bf16[128,512]{1,0:T(8,128)(2,1)}, f32[5,8,128]{2,1,0:T(8,128)}) custom-call(s32[1]{0:T(128)} %copy.21.start_ref, bf16[128,4096]{1,0:T(8,128)(2,1)} %bitcast.13, bf16[128,512]{1,0:T(8,128)(2,1)} %bitcast.17, bf16[128,512]{1,0:T(8,128)(2,1)} %bitcast.18, ...), custom_call_target="tpu_custom_call" | custom-call | tf_op jit(solution)/shard_map/attend/pallas_call | solution.py:288
  84.2 0.7 reshape.32
  85.0 0.6 pad.4.x_ref
  85.6 28.2 %bias_sums.1 = f32[8,8,128]{2,1,0:T(8,128)} custom-call(f32[8,8,128]{2,1,0:T(8,128)} %pad.4.x_ref), custom_call_target="tpu_custom_call" | custom-call | tf_op jit(solution)/shard_map/bias_sums/pallas_call | solution.py:327
  113.8 0.8 reshape.33
  114.6 0.6 fusion.1
  115.2 0.6 slice.16
  115.8 2.4 %copy.22 = bf16[1,128,4096]{2,1,0:T(8,128)(2,1)} copy(bf16[1,128,4096]{2,1,0:T(8,128)(2,1)} %bitcast.16) | data formatting | bytes 2097152
  118.2 0.0 copy-done
  118.2 1.0 copy.23
  119.1 0.1 copy-done.2
  119.2 0.7 copy.24
  119.9 0.3 copy-done.1
  120.2 0.7 copy.25
  (6 shorter events, 0.0 us)
Async XLA Ops:
  1.3 2.0 %copy-start.3 = (bf16[4096]{0:T(1024)(128)(2,1)S(1)}, bf16[4096]{0:T(1024)(128)(2,1)}, u32[]{:S(2)}) copy-start(bf16[4096]{0:T(1024)(128)(2,1)} %param.15) | copy-start | bytes 24580
  1.3 0.7 copy-start.4
  2.0 0.7 copy-start.5
  115.8 2.4 %copy-start = (bf16[128,4096]{1,0:T(8,128)(2,1)S(1)}, bf16[128,4096]{1,0:T(8,128)(2,1)}, u32[]{:S(2)}) copy-start(bf16[128,4096]{1,0:T(8,128)(2,1)} %get-tuple-element.13) | copy-start | bytes 3145732
  118.2 1.0 copy-start.2
  119.2 1.0 copy-start.1

commit v2 on v1

v2 whole, which is shorter than its diff:
```python
import functools

import jax
import jax.numpy as jnp
import numpy as np
from jax import lax
from jax.experimental import pallas as pl
from jax.experimental.pallas import tpu as pltpu
from jax.sharding import PartitionSpec as P

HQ = 32
KV = 4
HD = 128
GROUP = 8
SUMS = HQ + 2 * KV
SCALE = float(HD**-0.5)
EXP2_SCALE = float(np.log2(np.e) * HD**-0.5)
MESH = pl.DeviceIdType.MESH
f32 = jnp.float32
bf16 = jnp.bfloat16


def dot(a, b, contract_a, contract_b):
    return lax.dot_general(
        a, b, (((contract_a,), (contract_b,)), ((), ())), preferred_element_type=f32
    )


def turn(x):
    return pltpu.roll(x, HD // 2, axis=1)


def attend_kernel(
    n, inner, outer,
    start_ref, bias_ref, freq_ref, q_ref, k_ref, v_ref, ck_ref, cv_ref, do_ref,
    out_ref, gq_ref, gk_ref, gv_ref, sums_ref,
    kv, rsend, rrecv, q_s, do_s, s_ref, p_ref, mask_ref, stat, norm, acc, q_t, do_t, do_n, cos_s, sin_s,
    sum_a, sum_b, sum_c,
    kv_send, kv_recv, r_send, r_recv, a_send, a_recv, b_send, b_recv, c_send, c_recv,
):
    me, mine = lax.axis_index("seq"), lax.axis_index("dp")
    tokens = q_ref.shape[0]
    keys = n * tokens
    rows = GROUP * tokens
    ring = n // 2
    y, z = me // 2, lax.rem(me, 2)

    def place(dy, dz):
        return lax.rem(y + dy, ring) * 2 + lax.rem(z + dz, 2)

    up, down, far = place(1, 0), place(ring - 1, 0), place(2, 0)
    side, side_up, side_down, side_far = place(0, 1), place(1, 1), place(ring - 1, 1), place(2, 1)
    block, lane = mine // inner, lax.rem(mine, inner)

    barrier = pltpu.get_barrier_semaphore()

    def greet(device):
        pl.semaphore_signal(barrier, inc=1, device_id=device, device_id_type=MESH)

    def greet_seq(i, _):
        greet({"seq": lax.rem(me + i, n)})
        return 0

    def greet_inner(i, _):
        greet({"dp": block * inner + lax.rem(lane + i, inner)})
        return 0

    def greet_outer(i, _):
        greet({"dp": lax.rem(block + i, outer) * inner + lane})
        return 0

    lax.fori_loop(1, n, greet_seq, 0)
    lax.fori_loop(1, inner, greet_inner, 0)
    lax.fori_loop(1, outer, greet_outer, 0)

    flip = jnp.where(lax.broadcasted_iota(jnp.int32, (1, HD), 1) < HD // 2, -1.0, 1.0)

    def table(owner):
        at = pl.ds(pl.multiple_of(owner * tokens, tokens), tokens)
        position = start_ref[0] + owner * tokens + lax.broadcasted_iota(jnp.int32, (tokens, HD), 0)
        angle = position.astype(f32) * freq_ref[...]
        cos_s[at, :] = jnp.cos(angle)
        sin_s[at, :] = jnp.sin(angle) * flip

    table(me)
    own_rows = pl.ds(pl.multiple_of(me * tokens, tokens), tokens)
    cosine, sine = cos_s[own_rows, :], sin_s[own_rows, :]
    for h in range(KV):
        cols = slice(h * HD, (h + 1) * HD)
        x = k_ref[:, cols].astype(f32) + bias_ref[HQ + h : HQ + h + 1, :]
        kv[h, 0, 1, me] = (x * cosine + turn(x) * sine).astype(bf16)
        kv[h, 1, 1, me] = (v_ref[:, cols].astype(f32) + bias_ref[HQ + KV + h : HQ + KV + h + 1, :]).astype(bf16)
        kv[h, 0, 0, me] = ck_ref[:, cols]
        kv[h, 1, 0, me] = cv_ref[:, cols]

    pl.semaphore_wait(barrier, n + inner + outer - 3)

    def kv_copy(h, half, owner, peer, slot):
        part = kv.at[h, half, :, owner]
        return pltpu.make_async_remote_copy(
            src_ref=part, dst_ref=part, send_sem=kv_send.at[h, half, slot], recv_sem=kv_recv.at[h, half, owner],
            device_id={"seq": peer}, device_id_type=MESH,
        )

    def arrived(h, half, owner):
        kv_copy(h, half, owner, owner, 0).wait_recv()

    def r_copy(h, source, peer):
        return pltpu.make_async_remote_copy(
            src_ref=rsend.at[h, :, peer], dst_ref=rrecv.at[h, :, source],
            send_sem=r_send.at[h, peer], recv_sem=r_recv.at[h, source],
            device_id={"seq": peer}, device_id_type=MESH,
        )

    def send_own(h):
        for half in range(2):
            kv_copy(h, half, me, side, 0).start()
            kv_copy(h, half, me, up, 1).start()
            kv_copy(h, half, me, down, 2).start()

    def relay_near(h):
        for half in range(2):
            arrived(h, half, side)
            kv_copy(h, half, side, up, 3).start()
            kv_copy(h, half, side, down, 4).start()
            if half == 0:
                arrived(h, 0, down)
                kv_copy(h, 0, down, up, 5).start()
            else:
                arrived(h, 1, up)
                kv_copy(h, 1, up, down, 5).start()

    def relay_far(h):
        for half in range(2):
            arrived(h, half, far)
            kv_copy(h, half, far, side, 6).start()

    def await_half(h, half):
        arrived(h, half, up if half == 0 else down)
        for owner in (side_up, side_down, side_far):
            arrived(h, half, owner)

    def load_queries(h, _):
        for g in range(GROUP):
            cols = pl.ds(pl.multiple_of((h * GROUP + g) * HD, HD), HD)
            x = q_ref[:, cols].astype(f32) + bias_ref[pl.ds(h * GROUP + g, 1), :]
            q_s[h, g * tokens : (g + 1) * tokens, :] = (x * cosine + turn(x) * sine).astype(bf16)
            do_s[h, g * tokens : (g + 1) * tokens, :] = do_ref[:, cols]
        return 0

    send_own(0)
    lax.fori_loop(0, KV, load_queries, 0)
    relay_near(0)
    send_own(1)

    row = lax.broadcasted_iota(jnp.int32, (tokens, keys), 0)
    col = lax.broadcasted_iota(jnp.int32, (tokens, keys), 1)
    mask_ref[0] = jnp.where(col < start_ref[0], 0.0, -1e30)
    mask_ref[1] = jnp.where(col <= row + me * tokens, 0.0, -1e30)

    def more_tables(i, _):
        table(lax.rem(me + i, n))
        return 0

    relay_far(0)
    lax.fori_loop(1, n, more_tables, 0)

    def finish(h):
        cols = pl.ds(pl.multiple_of(h * HD, HD), HD)

        def gather(source, total):
            r_copy(h, source, source).wait_recv()
            return total + rrecv[h, :, source].astype(f32)

        total = lax.fori_loop(me + 1, n, gather, rsend[h, :, me].astype(f32))
        gk_ref[:, cols] = (total[0] * cosine - turn(total[0]) * sine).astype(bf16)
        gv_ref[:, cols] = total[1].astype(bf16)

    def head(h, _):
        await_half(h, 0)
        q_t[...] = q_s[h].T
        stat[...] = jnp.full(stat.shape, -3e38, f32)

        def score(part, _):
            s = dot(q_s[h], kv[h, 0, part].reshape(keys, HD), 1, 1)
            s = (s.reshape(GROUP, tokens, keys) + mask_ref[part][None]).reshape(rows, keys)
            s_ref[part] = s
            m = stat[...]
            for t in range(keys // HD):
                m = jnp.maximum(m, s[:, t * HD : (t + 1) * HD])
            stat[...] = m
            return 0

        lax.fori_loop(0, 2, score, 0)

        @pl.when(h + 1 < KV)
        def _():
            relay_near(h + 1)

        stat[...] = jnp.broadcast_to(jnp.max(stat[...], axis=1, keepdims=True), stat.shape)
        norm[...] = jnp.zeros(norm.shape, f32)
        acc[...] = jnp.zeros(acc.shape, f32)
        await_half(h, 1)

        def weigh(part, _):
            m = stat[...]
            pieces = [
                jnp.exp2((s_ref[part, :, t * HD : (t + 1) * HD] - m) * EXP2_SCALE)
                for t in range(keys // HD)
            ]
            norm[...] += functools.reduce(lambda a, b: a + b, pieces)
            p = jnp.concatenate([x.astype(bf16) for x in pieces], axis=1)
            p_ref[part] = p
            acc[...] += dot(p, kv[h, 1, part].reshape(keys, HD), 1, 0)
            return 0

        lax.fori_loop(0, 2, weigh, 0)

        @pl.when(h + 1 < KV)
        def _():
            relay_far(h + 1)

        @pl.when(h + 2 < KV)
        def _():
            send_own(h + 2)

        inverse = 1.0 / jnp.sum(norm[...], axis=1, keepdims=True)
        out = (acc[...] * inverse).astype(bf16)
        for g in range(GROUP):
            cols = pl.ds(pl.multiple_of((h * GROUP + g) * HD, HD), HD)
            out_ref[:, cols] = out[g * tokens : (g + 1) * tokens]
        scaled = (do_s[h].astype(f32) * inverse).astype(bf16)
        do_n[...] = scaled
        do_t[...] = scaled.T
        delta = jnp.sum(scaled.astype(f32) * out.astype(f32), axis=1, keepdims=True)
        stat[...] = jnp.broadcast_to(delta, stat.shape)
        acc[...] = jnp.zeros(acc.shape, f32)

        def score_grad(part):
            dp = dot(do_n[...], kv[h, 1, part].reshape(keys, HD), 1, 1)
            delta = stat[...]
            ds = jnp.concatenate(
                [
                    (
                        (dp[:, t * HD : (t + 1) * HD] - delta)
                        * p_ref[part, :, t * HD : (t + 1) * HD].astype(f32)
                    ).astype(bf16)
                    for t in range(keys // HD)
                ],
                axis=1,
            )
            acc[...] += dot(ds, kv[h, 0, part].reshape(keys, HD), 1, 0)
            return ds

        ds = score_grad(1)
        dk = dot(q_t[...], ds, 1, 0).T * SCALE
        dv = dot(do_t[...], p_ref[1], 1, 0).T
        rsend[h, 0] = dk.astype(bf16).reshape(n, tokens, HD)
        rsend[h, 1] = dv.astype(bf16).reshape(n, tokens, HD)

        def send_back(peer, _):
            r_copy(h, me, peer).start()
            return 0

        lax.fori_loop(0, me, send_back, 0)
        gk = dk * cos_s[...] - turn(dk) * sin_s[...]
        sum_a[me, pl.ds(HQ + h, 1), :] = jnp.sum(gk, axis=0, keepdims=True)
        sum_a[me, pl.ds(HQ + KV + h, 1), :] = jnp.sum(dv, axis=0, keepdims=True)
        score_grad(0)
        dq = (acc[...] * SCALE).astype(bf16).astype(f32)
        sums = []
        for g in range(GROUP):
            cols = pl.ds(pl.multiple_of((h * GROUP + g) * HD, HD), HD)
            x = dq[g * tokens : (g + 1) * tokens]
            gq = x * cosine - turn(x) * sine
            gq_ref[:, cols] = gq.astype(bf16)
            sums.append(jnp.sum(gq, axis=0, keepdims=True))
        sum_a[me, pl.ds(pl.multiple_of(h * GROUP, GROUP), GROUP), :] = jnp.concatenate(sums, axis=0)

        @pl.when(h > 0)
        def _():
            finish(h - 1)

        return 0

    lax.fori_loop(0, KV, head, 0)

    def exchange(size, index, device, buffer, send, recv):
        def copy(owner, peer):
            return pltpu.make_async_remote_copy(
                src_ref=buffer.at[owner], dst_ref=buffer.at[owner], send_sem=send.at[peer], recv_sem=recv.at[owner],
                device_id=device(peer), device_id_type=MESH,
            )

        def begin(i, _):
            copy(index, lax.rem(index + i, size)).start()
            return 0

        def arrive(i, _):
            peer = lax.rem(index + i, size)
            copy(peer, peer).wait_recv()
            return 0

        def leave(i, _):
            copy(index, lax.rem(index + i, size)).wait_send()
            return 0

        lax.fori_loop(1, size, begin, 0)
        return (
            lambda: lax.fori_loop(1, size, arrive, 0),
            lambda: lax.fori_loop(1, size, leave, 0),
        )

    arrive_a, leave_a = exchange(n, me, lambda p: {"seq": p}, sum_a, a_send, a_recv)
    finish(KV - 1)
    arrive_a()
    sum_b[lane] = jnp.sum(sum_a[...], axis=0)
    arrive_b, leave_b = exchange(inner, lane, lambda p: {"dp": block * inner + p}, sum_b, b_send, b_recv)
    arrive_b()
    sum_c[block] = jnp.sum(sum_b[...], axis=0)
    arrive_c, leave_c = exchange(outer, block, lambda p: {"dp": p * inner + lane}, sum_c, c_send, c_recv)

    def drain_head(h, _):
        for half in range(2):
            for slot, peer in enumerate((side, up, down, up, down, up if half == 0 else down, side)):
                kv_copy(h, half, me, peer, slot).wait_send()

        def drain_r(peer, _):
            r_copy(h, me, peer).wait_send()
            return 0

        return lax.fori_loop(0, me, drain_r, 0)

    lax.fori_loop(0, KV, drain_head, 0)
    leave_a()
    leave_b()
    arrive_c()
    sums_ref[...] = jnp.sum(sum_c[...], axis=0)
    leave_c()


def body(n, m, q_proj, k_proj, v_proj, cache_k, cache_v, bias_q, bias_k, bias_v, start, dout):
    tokens = q_proj.shape[1]
    keys, rows = n * tokens, GROUP * tokens
    inner = 8
    outer = m // inner
    half = HD // 2
    freqs = np.exp(-(2.0 * np.arange(half) / HD) * np.log(1e6)).astype(np.float32)
    freqs = jnp.asarray(np.concatenate([freqs, freqs])[None])
    bias = jnp.concatenate([bias_q, bias_k, bias_v]).astype(f32).reshape(SUMS, HD)
    vmem = pl.BlockSpec(memory_space=pltpu.VMEM)
    dma = pltpu.SemaphoreType.DMA
    out, grad_q, grad_k, grad_v, total = pl.pallas_call(
        functools.partial(attend_kernel, n, inner, outer),
        out_shape=[
            jax.ShapeDtypeStruct((tokens, HQ * HD), bf16),
            jax.ShapeDtypeStruct((tokens, HQ * HD), bf16),
            jax.ShapeDtypeStruct((tokens, KV * HD), bf16),
            jax.ShapeDtypeStruct((tokens, KV * HD), bf16),
            jax.ShapeDtypeStruct((SUMS, HD), f32),
        ],
        in_specs=[pl.BlockSpec(memory_space=pltpu.SMEM)] + [vmem] * 8,
        out_specs=[vmem] * 5,
        scratch_shapes=[
            pltpu.VMEM((KV, 2, 2, n, tokens, HD), bf16),
            pltpu.VMEM((KV, 2, n, tokens, HD), bf16),
            pltpu.VMEM((KV, 2, n, tokens, HD), bf16),
            pltpu.VMEM((KV, rows, HD), bf16),
            pltpu.VMEM((KV, rows, HD), bf16),
            pltpu.VMEM((2, rows, keys), f32),
            pltpu.VMEM((2, rows, keys), bf16),
            pltpu.VMEM((2, tokens, keys), f32),
            pltpu.VMEM((rows, HD), f32),
            pltpu.VMEM((rows, HD), f32),
            pltpu.VMEM((rows, HD), f32),
            pltpu.VMEM((HD, rows), bf16),
            pltpu.VMEM((HD, rows), bf16),
            pltpu.VMEM((rows, HD), bf16),
            pltpu.VMEM((keys, HD), f32),
            pltpu.VMEM((keys, HD), f32),
            pltpu.VMEM((n, SUMS, HD), f32),
            pltpu.VMEM((inner, SUMS, HD), f32),
            pltpu.VMEM((outer, SUMS, HD), f32),
            dma((KV, 2, 7)),
            dma((KV, 2, n)),
            dma((KV, n)),
            dma((KV, n)),
            dma((n,)),
            dma((n,)),
            dma((inner,)),
            dma((inner,)),
            dma((outer,)),
            dma((outer,)),
        ],
        compiler_params=pltpu.CompilerParams(collective_id=0, has_side_effects=True, vmem_limit_bytes=VMEM_LIMIT),
        name="attend",
    )(start, bias, freqs, q_proj[0], k_proj[0], v_proj[0], cache_k[0], cache_v[0], dout[0])
    total = total.reshape(SUMS * HD)
    split = HQ * HD
    return (
        out[None], grad_q[None], grad_k[None], grad_v[None],
        total[:split], total[split : split + KV * HD], total[split + KV * HD :],
    )


VMEM_LIMIT = 44 << 20


def solution(mesh):
    n, m = mesh.shape["seq"], mesh.shape["dp"]
    tokens = P("dp", "seq", None)
    return jax.shard_map(
        functools.partial(body, n, m),
        mesh=mesh,
        in_specs=(tokens, tokens, tokens, tokens, tokens, P(), P(), P(), P("dp"), tokens),
        out_specs=(tokens, tokens, tokens, tokens, P(), P(), P()),
        check_vma=False,
    )
```

time: 121 us -> 99.2 us (0.82)
  Pallas kernels: 108 us -> 85.6 us
    pallas_call x2 -> x1, Pallas kernels: 108 us -> 85.6 us  [body(): pl.pallas_call(functools.partial(attend_kernel, n, inner, outer), out_sha...]
    unnamed x16 -> x24, local copies, waits for them, and re-layouts: 5.78 us -> 10.6 us
    broadcast_in_dim x3 -> x0, local copies, waits for them, and re-layouts: 1.78 us -> none  [the longest x1 0.62 us: body(): bias_q[None]]
    reshape x2 -> x0, local copies, waits for them, and re-layouts: 1.49 us -> none  [the longest x1 0.76 us: body(): total = total[:, :slots].reshape((KV + 1) * GROUP * HD)]
where the time goes in v2:
time: 99.2 us; the launch traced here: 98.8 us
  Pallas kernels  85.6 us (86%)
  local copies, waits for them, and re-layouts  11.8 us (12%)
  between operations  1.34 us (1%)
    pallas_call x1, Pallas kernels, body(): pl.pallas_call(functools.partial(attend_kernel, n, inner, outer), out_sha...  85.6 us
    unnamed x24, local copies, waits for them, and re-layouts  10.6 us

profile of v2, /device:TPU:1, one launch (start us, length us, event | category | flops | bytes accessed | tf_op | source)
XLA Modules:
  0.0 98.8 jit_solution(4541842982328409541)
XLA Ops:
  0.6 0.0 copy-start.7
  1.3 0.0 copy-start.9
  1.3 0.0 copy-start.8
  1.3 0.0 copy-done.7
  1.3 0.7 copy-done.9
  2.0 0.0 copy-done.8
  2.0 0.0 copy-start.6
  2.0 0.6 copy-done.6
  2.7 0.0 copy-start
  2.7 1.2 %copy-done = bf16[1,128,4096]{2,1,0:T(8,128)(2,1)S(1)} copy-done((bf16[1,128,4096]{2,1,0:T(8,128)(2,1)S(1)}, bf16[1,128,4096]{2,1,0:T(8,128)(2,1)}, u32[]{:S(2)}) %copy-start) | copy-done | bytes 1048600
  3.9 0.0 copy-start.1
  3.9 1.2 %copy-done.1 = bf16[1,128,4096]{2,1,0:T(8,128)(2,1)S(1)} copy-done((bf16[1,128,4096]{2,1,0:T(8,128)(2,1)S(1)}, bf16[1,128,4096]{2,1,0:T(8,128)(2,1)}, u32[]{:S(2)}) %copy-start.1) | copy-done | bytes 1048600
  5.1 0.9 copy-done.2
  6.0 0.0 copy-start.3
  6.0 0.9 copy-done.3
  6.9 0.9 copy-done.4
  7.8 0.9 copy-done.5
  8.7 85.6 %attend.1 = (bf16[128,4096]{1,0:T(8,128)(2,1)S(1)}, bf16[128,4096]{1,0:T(8,128)(2,1)S(1)}, bf16[128,512]{1,0:T(8,128)(2,1)S(1)}, bf16[128,512]{1,0:T(8,128)(2,1)S(1)}, f32[40,128]{1,0:T(8,128)S(1)}) custom-call(s32[1]{0:T(128)S(6)} %copy.22.start_ref, f32[40,128]{1,0:T(8,128)S(1)} %fusion.bias_ref, f32[1,128]{1,0:T(1,128)S(1)} %copy-done.6, ...), custom_call_target="tpu_custom_call" | custom-call | tf_op jit(solution)/shard_map/attend/pallas_call | solution.py:353
  94.3 0.6 slice_bitcast_fusion.1
  94.9 0.6 slice_bitcast_fusion
  95.5 1.0 copy.23
  96.5 1.0 copy.24
  97.5 0.7 copy.25
  98.1 0.7 copy.26
  (4 shorter events, 0.0 us)
Async XLA Ops:
  0.6 0.7 copy-start.7
  1.3 0.7 copy-start.9
  1.3 0.7 copy-start.8
  2.0 0.7 copy-start.6
  2.7 1.2 %copy-start = (bf16[1,128,4096]{2,1,0:T(8,128)(2,1)S(1)}, bf16[1,128,4096]{2,1,0:T(8,128)(2,1)}, u32[]{:S(2)}) copy-start(bf16[1,128,4096]{2,1,0:T(8,128)(2,1)} %param.11) | copy-start | bytes 3145732
  3.9 1.2 %copy-start.1 = (bf16[1,128,4096]{2,1,0:T(8,128)(2,1)S(1)}, bf16[1,128,4096]{2,1,0:T(8,128)(2,1)}, u32[]{:S(2)}) copy-start(bf16[1,128,4096]{2,1,0:T(8,128)(2,1)} %param.20) | copy-start | bytes 3145732
  5.1 0.9 copy-start.2
  6.0 0.9 copy-start.3
  6.9 0.9 copy-start.4
  7.8 0.9 copy-start.5

commit v3 on v2

v3 whole, which is shorter than its diff:
```python
import functools

import jax
import jax.numpy as jnp
import numpy as np
from jax import lax
from jax.experimental import pallas as pl
from jax.experimental.pallas import tpu as pltpu
from jax.sharding import PartitionSpec as P

HQ = 32
KV = 4
HD = 128
GROUP = 8
SUMS = HQ + 2 * KV
SLOTS = 16
SCALE = float(HD**-0.5)
EXP2_SCALE = float(np.log2(np.e) * HD**-0.5)
MESH = pl.DeviceIdType.MESH
f32 = jnp.float32
bf16 = jnp.bfloat16


def dot(a, b, contract_a, contract_b):
    return lax.dot_general(
        a, b, (((contract_a,), (contract_b,)), ((), ())), preferred_element_type=f32
    )


def turn(x):
    return pltpu.roll(x, HD // 2, axis=1)


def attend_kernel(
    n, inner, outer,
    start_ref, bias_ref, freq_ref, q_ref, k_ref, v_ref, ck_ref, cv_ref, do_ref,
    out_ref, gq_ref, gk_ref, gv_ref, sums_ref,
    q_in, k_in, v_in, kv, rsend, rrecv, q_s, do_s, s_ref, p_ref, mask_ref, stat, norm, acc, q_t, do_t, do_n,
    cos_s, sin_s, sum_a, sum_b, sum_c,
    in_sem, cache_sem, do_sem, kv_send, kv_recv, r_send, r_recv,
    a_send, a_recv, b_send, b_recv, c_send, c_recv,
):
    me, mine = lax.axis_index("seq"), lax.axis_index("dp")
    tokens = q_ref.shape[0]
    keys = n * tokens
    rows = GROUP * tokens
    ring = n // 2
    y, z = me // 2, lax.rem(me, 2)

    def place(dy, dz):
        return lax.rem(y + dy, ring) * 2 + lax.rem(z + dz, 2)

    up, down, far = place(1, 0), place(ring - 1, 0), place(2, 0)
    side, side_up, side_down, side_far = place(0, 1), place(1, 1), place(ring - 1, 1), place(2, 1)
    block, lane = mine // inner, lax.rem(mine, inner)

    def head_cols(h):
        return pl.ds(pl.multiple_of(h * HD, HD), HD)

    fetch_k = pltpu.make_async_copy(k_ref, k_in, in_sem.at[0])
    fetch_v = pltpu.make_async_copy(v_ref, v_in, in_sem.at[1])
    fetch_q = pltpu.make_async_copy(q_ref, q_in, in_sem.at[2])

    def fetch_cache(h, half):
        source = (ck_ref, cv_ref)[half]
        return pltpu.make_async_copy(source.at[:, head_cols(h)], kv.at[h, half, 0, me], cache_sem.at[h, half])

    def fetch_do(h, g):
        target = do_s.at[h, pl.ds(pl.multiple_of(g * tokens, tokens), tokens), :]
        return pltpu.make_async_copy(do_ref.at[:, head_cols(h * GROUP + g)], target, do_sem.at[h, g])

    fetch_k.start()
    fetch_v.start()

    def begin_cache(h, _):
        fetch_cache(h, 0).start()
        fetch_cache(h, 1).start()
        return 0

    lax.fori_loop(0, KV, begin_cache, 0)
    fetch_q.start()

    barrier = pltpu.get_barrier_semaphore()

    def greet(device):
        pl.semaphore_signal(barrier, inc=1, device_id=device, device_id_type=MESH)

    def greet_seq(i, _):
        greet({"seq": lax.rem(me + i, n)})
        return 0

    def greet_inner(i, _):
        greet({"dp": block * inner + lax.rem(lane + i, inner)})
        return 0

    def greet_outer(i, _):
        greet({"dp": lax.rem(block + i, outer) * inner + lane})
        return 0

    lax.fori_loop(1, n, greet_seq, 0)
    lax.fori_loop(1, inner, greet_inner, 0)
    lax.fori_loop(1, outer, greet_outer, 0)

    flip = jnp.where(lax.broadcasted_iota(jnp.int32, (1, HD), 1) < HD // 2, -1.0, 1.0)

    def table(owner):
        at = pl.ds(pl.multiple_of(owner * tokens, tokens), tokens)
        position = start_ref[0] + owner * tokens + lax.broadcasted_iota(jnp.int32, (tokens, HD), 0)
        angle = position.astype(f32) * freq_ref[...]
        cos_s[at, :] = jnp.cos(angle)
        sin_s[at, :] = jnp.sin(angle) * flip

    table(me)
    own_rows = pl.ds(pl.multiple_of(me * tokens, tokens), tokens)
    cosine, sine = cos_s[own_rows, :], sin_s[own_rows, :]
    fetch_k.wait()
    fetch_v.wait()
    for h in range(KV):
        cols = slice(h * HD, (h + 1) * HD)
        x = k_in[:, cols].astype(f32) + bias_ref[HQ + h : HQ + h + 1, :]
        kv[h, 0, 1, me] = (x * cosine + turn(x) * sine).astype(bf16)
        kv[h, 1, 1, me] = (v_in[:, cols].astype(f32) + bias_ref[HQ + KV + h : HQ + KV + h + 1, :]).astype(bf16)

    pl.semaphore_wait(barrier, n + inner + outer - 3)

    def kv_copy(h, part, owner, peer, slot):
        block = kv.at[h, :, part, owner]
        return pltpu.make_async_remote_copy(
            src_ref=block, dst_ref=block,
            send_sem=kv_send.at[h, part, slot], recv_sem=kv_recv.at[h, part, owner],
            device_id={"seq": peer}, device_id_type=MESH,
        )

    top = ring - 1
    routes = (
        (me, side, jnp.logical_or(z == 0, y < top)),
        (me, up, y < top),
        (me, down, y == 0),
        (side, up, y < top),
        (side, down, y <= 1),
        (down, up, jnp.logical_and(y >= 1, y < top)),
        (side_up, down, jnp.logical_or(y == 0, y == top)),
    )

    def both_parts(needed, step):
        step(0)

        @pl.when(needed)
        def _():
            step(1)

    def send(h, *slots):
        for slot in slots:
            owner, peer, needed = routes[slot]
            both_parts(needed, lambda part: kv_copy(h, part, owner, peer, slot).start())

    def arrived(h, owner, needed):
        both_parts(needed, lambda part: kv_copy(h, part, owner, owner, 0).wait_recv())

    def send_own(h):
        send(h, 0, 1, 2)

    def relay_near(h):
        arrived(h, side, jnp.logical_or(z == 1, y < top))
        send(h, 3, 4)
        arrived(h, down, y >= 1)
        send(h, 5)

    def relay_far(h):
        arrived(h, side_up, jnp.logical_or(y == top, y == 0))
        send(h, 6)

    def await_rest(h):
        arrived(h, up, y == top)
        arrived(h, side_down, y >= 1)
        arrived(h, far, y >= 2)
        arrived(h, side_far, y >= 2)

    def direct(step):
        for part in range(2):

            def one(i, _):
                peer = lax.rem(me + i, n)
                pl.when(jnp.logical_or(part == 0, peer > me))(lambda: step(kv_copy(0, part, me, peer, i - 1)))
                return 0

            lax.fori_loop(1, n, one, 0)

    def await_direct():
        def one(i, _):
            owner = lax.rem(me + i, n)
            arrived(0, owner, owner < me)
            return 0

        lax.fori_loop(1, n, one, 0)

    def r_copy(h, source, peer):
        return pltpu.make_async_remote_copy(
            src_ref=rsend.at[h, peer], dst_ref=rrecv.at[h, source],
            send_sem=r_send.at[h, peer], recv_sem=r_recv.at[h, source],
            device_id={"seq": peer}, device_id_type=MESH,
        )

    def load_queries(h, _):
        for g in range(GROUP):
            cols = pl.ds(pl.multiple_of((h * GROUP + g) * HD, HD), HD)
            x = q_in[:, cols].astype(f32) + bias_ref[pl.ds(h * GROUP + g, 1), :]
            q_s[h, g * tokens : (g + 1) * tokens, :] = (x * cosine + turn(x) * sine).astype(bf16)
        return 0

    def await_cache(h, _):
        fetch_cache(h, 0).wait()
        fetch_cache(h, 1).wait()
        return 0

    lax.fori_loop(0, KV, await_cache, 0)
    direct(lambda copy: copy.start())
    send_own(1)

    def begin_do(i, _):
        fetch_do(i // GROUP, lax.rem(i, GROUP)).start()
        return 0

    lax.fori_loop(0, KV * GROUP, begin_do, 0)
    fetch_q.wait()
    lax.fori_loop(0, KV, load_queries, 0)

    row = lax.broadcasted_iota(jnp.int32, (tokens, keys), 0)
    col = lax.broadcasted_iota(jnp.int32, (tokens, keys), 1)
    mask_ref[0] = jnp.where(col < start_ref[0], 0.0, -1e30)
    mask_ref[1] = jnp.where(col <= row + me * tokens, 0.0, -1e30)

    def more_tables(i, _):
        table(lax.rem(me + i, n))
        return 0

    lax.fori_loop(1, n, more_tables, 0)

    def finish(h):
        cols = pl.ds(pl.multiple_of(h * HD, HD), HD)

        def gather(source, total):
            r_copy(h, source, source).wait_recv()
            return total + rrecv[h, source].astype(f32)

        total = lax.fori_loop(me + 1, n, gather, rsend[h, me].astype(f32))
        gk_ref[:, cols] = (total[0] * cosine - turn(total[0]) * sine).astype(bf16)
        gv_ref[:, cols] = total[1].astype(bf16)

    early, late = slice(0, KV - 1), slice(KV - 1, KV)

    def exchange(size, index, device, buffer, send_sem, recv_sem):
        def copy(which, owner, peer):
            block = buffer.at[owner, (early, late)[which]]
            return pltpu.make_async_remote_copy(
                src_ref=block, dst_ref=block, send_sem=send_sem.at[which, peer], recv_sem=recv_sem.at[which, owner],
                device_id=device(peer), device_id_type=MESH,
            )

        def begin(which):
            def one(i, _):
                copy(which, index, lax.rem(index + i, size)).start()
                return 0

            lax.fori_loop(1, size, one, 0)

        def arrive(which):
            def one(i, _):
                peer = lax.rem(index + i, size)
                copy(which, peer, peer).wait_recv()
                return 0

            lax.fori_loop(1, size, one, 0)
            return jnp.sum(buffer[:, (early, late)[which]], axis=0)

        def leave(which):
            def one(i, _):
                copy(which, index, lax.rem(index + i, size)).wait_send()
                return 0

            lax.fori_loop(1, size, one, 0)

        return begin, arrive, leave

    begin_a, arrive_a, leave_a = exchange(n, me, lambda p: {"seq": p}, sum_a, a_send, a_recv)
    begin_b, arrive_b, leave_b = exchange(inner, lane, lambda p: {"dp": block * inner + p}, sum_b, b_send, b_recv)
    begin_c, arrive_c, leave_c = exchange(outer, block, lambda p: {"dp": p * inner + lane}, sum_c, c_send, c_recv)

    def head(h, _):
        last = h == KV - 1

        @pl.when(last)
        def _():
            begin_a(0)

        @pl.when(h == 0)
        def _():
            await_direct()

        @pl.when(h > 0)
        def _():
            await_rest(h)

        q_t[...] = q_s[h].T
        stat[...] = jnp.full(stat.shape, -3e38, f32)

        def score(part, _):
            s = dot(q_s[h], kv[h, 0, part].reshape(keys, HD), 1, 1)
            s = (s.reshape(GROUP, tokens, keys) + mask_ref[part][None]).reshape(rows, keys)
            s_ref[part] = s
            m = stat[...]
            for t in range(keys // HD):
                m = jnp.maximum(m, s[:, t * HD : (t + 1) * HD])
            stat[...] = m
            return 0

        lax.fori_loop(0, 2, score, 0)

        @pl.when(h + 1 < KV)
        def _():
            relay_near(h + 1)


        stat[...] = jnp.broadcast_to(jnp.max(stat[...], axis=1, keepdims=True), stat.shape)
        norm[...] = jnp.zeros(norm.shape, f32)
        acc[...] = jnp.zeros(acc.shape, f32)

        def weigh(part, _):
            m = stat[...]
            pieces = [
                jnp.exp2((s_ref[part, :, t * HD : (t + 1) * HD] - m) * EXP2_SCALE)
                for t in range(keys // HD)
            ]
            norm[...] += functools.reduce(lambda a, b: a + b, pieces)
            p = jnp.concatenate([x.astype(bf16) for x in pieces], axis=1)
            p_ref[part] = p
            acc[...] += dot(p, kv[h, 1, part].reshape(keys, HD), 1, 0)
            return 0

        lax.fori_loop(0, 2, weigh, 0)

        @pl.when(h + 1 < KV)
        def _():
            relay_far(h + 1)

        @pl.when(h + 2 < KV)
        def _():
            send_own(h + 2)

        @pl.when(last)
        def _():
            sum_b[lane, early] = arrive_a(0)
            begin_b(0)

        def await_do(g, _):
            fetch_do(h, g).wait()
            return 0

        lax.fori_loop(0, GROUP, await_do, 0)
        inverse = 1.0 / jnp.sum(norm[...], axis=1, keepdims=True)
        out = (acc[...] * inverse).astype(bf16)
        for g in range(GROUP):
            cols = pl.ds(pl.multiple_of((h * GROUP + g) * HD, HD), HD)
            out_ref[:, cols] = out[g * tokens : (g + 1) * tokens]
        scaled = (do_s[h].astype(f32) * inverse).astype(bf16)
        do_n[...] = scaled
        do_t[...] = scaled.T
        delta = jnp.sum(scaled.astype(f32) * out.astype(f32), axis=1, keepdims=True)
        stat[...] = jnp.broadcast_to(delta, stat.shape)
        acc[...] = jnp.zeros(acc.shape, f32)

        def score_grad(part):
            dp = dot(do_n[...], kv[h, 1, part].reshape(keys, HD), 1, 1)
            delta = stat[...]
            ds = jnp.concatenate(
                [
                    (
                        (dp[:, t * HD : (t + 1) * HD] - delta)
                        * p_ref[part, :, t * HD : (t + 1) * HD].astype(f32)
                    ).astype(bf16)
                    for t in range(keys // HD)
                ],
                axis=1,
            )
            acc[...] += dot(ds, kv[h, 0, part].reshape(keys, HD), 1, 0)
            return ds

        ds = score_grad(1)
        dk = dot(q_t[...], ds, 1, 0).T * SCALE
        dv = dot(do_t[...], p_ref[1], 1, 0).T
        for r in range(n):
            rsend[h, r, 0] = dk[r * tokens : (r + 1) * tokens].astype(bf16)
            rsend[h, r, 1] = dv[r * tokens : (r + 1) * tokens].astype(bf16)

        def send_back(peer, _):
            r_copy(h, me, peer).start()
            return 0

        lax.fori_loop(0, me, send_back, 0)
        gk = dk * cos_s[...] - turn(dk) * sin_s[...]
        key_sums = [jnp.sum(gk, axis=0, keepdims=True), jnp.sum(dv, axis=0, keepdims=True)]
        score_grad(0)
        dq = (acc[...] * SCALE).astype(bf16).astype(f32)
        sums = []
        for g in range(GROUP):
            cols = pl.ds(pl.multiple_of((h * GROUP + g) * HD, HD), HD)
            x = dq[g * tokens : (g + 1) * tokens]
            gq = x * cosine - turn(x) * sine
            gq_ref[:, cols] = gq.astype(bf16)
            sums.append(jnp.sum(gq, axis=0, keepdims=True))
        filler = jnp.zeros((SLOTS - GROUP - 2, HD), f32)
        sum_a[me, h] = jnp.concatenate(sums + key_sums + [filler], axis=0)

        @pl.when(h > 0)
        def _():
            finish(h - 1)

        return 0

    lax.fori_loop(0, KV, head, 0)

    begin_a(1)
    sum_c[block, early] = arrive_b(0)
    begin_c(0)
    sum_b[lane, late] = arrive_a(1)
    begin_b(1)
    finish(KV - 1)
    sum_c[block, late] = arrive_b(1)
    begin_c(1)

    def drain_head(h, _):
        for slot, (_owner, peer, needed) in enumerate(routes):
            both_parts(needed, lambda part: kv_copy(h, part, me, peer, slot).wait_send())
        return 0

    def drain_back(h, _):
        def one(peer, _):
            r_copy(h, me, peer).wait_send()
            return 0

        return lax.fori_loop(0, me, one, 0)

    direct(lambda copy: copy.wait_send())
    lax.fori_loop(1, KV, drain_head, 0)
    lax.fori_loop(0, KV, drain_back, 0)
    for which in range(2):
        leave_a(which)
        leave_b(which)
    sums_ref[early] = arrive_c(0)
    sums_ref[late] = arrive_c(1)
    leave_c(0)
    leave_c(1)


def body(n, m, q_proj, k_proj, v_proj, cache_k, cache_v, bias_q, bias_k, bias_v, start, dout):
    tokens = q_proj.shape[1]
    keys, rows = n * tokens, GROUP * tokens
    inner = 8
    outer = m // inner
    half = HD // 2
    freqs = np.exp(-(2.0 * np.arange(half) / HD) * np.log(1e6)).astype(np.float32)
    freqs = jnp.asarray(np.concatenate([freqs, freqs])[None])
    bias = jnp.concatenate([bias_q, bias_k, bias_v]).astype(f32).reshape(SUMS, HD)
    vmem = pl.BlockSpec(memory_space=pltpu.VMEM)
    dma = pltpu.SemaphoreType.DMA
    out, grad_q, grad_k, grad_v, total = pl.pallas_call(
        functools.partial(attend_kernel, n, inner, outer),
        out_shape=[
            jax.ShapeDtypeStruct((tokens, HQ * HD), bf16),
            jax.ShapeDtypeStruct((tokens, HQ * HD), bf16),
            jax.ShapeDtypeStruct((tokens, KV * HD), bf16),
            jax.ShapeDtypeStruct((tokens, KV * HD), bf16),
            jax.ShapeDtypeStruct((KV, SLOTS, HD), f32),
        ],
        in_specs=[pl.BlockSpec(memory_space=pltpu.SMEM), vmem, vmem] + [pl.BlockSpec(memory_space=pltpu.HBM)] * 6,
        out_specs=[vmem] * 5,
        scratch_shapes=[
            pltpu.VMEM((tokens, HQ * HD), bf16),
            pltpu.VMEM((tokens, KV * HD), bf16),
            pltpu.VMEM((tokens, KV * HD), bf16),
            pltpu.VMEM((KV, 2, 2, n, tokens, HD), bf16),
            pltpu.VMEM((KV, n, 2, tokens, HD), bf16),
            pltpu.VMEM((KV, n, 2, tokens, HD), bf16),
            pltpu.VMEM((KV, rows, HD), bf16),
            pltpu.VMEM((KV, rows, HD), bf16),
            pltpu.VMEM((2, rows, keys), f32),
            pltpu.VMEM((2, rows, keys), bf16),
            pltpu.VMEM((2, tokens, keys), f32),
            pltpu.VMEM((rows, HD), f32),
            pltpu.VMEM((rows, HD), f32),
            pltpu.VMEM((rows, HD), f32),
            pltpu.VMEM((HD, rows), bf16),
            pltpu.VMEM((HD, rows), bf16),
            pltpu.VMEM((rows, HD), bf16),
            pltpu.VMEM((keys, HD), f32),
            pltpu.VMEM((keys, HD), f32),
            pltpu.VMEM((n, KV, SLOTS, HD), f32),
            pltpu.VMEM((inner, KV, SLOTS, HD), f32),
            pltpu.VMEM((outer, KV, SLOTS, HD), f32),
            dma((3,)),
            dma((KV, 2)),
            dma((KV, GROUP)),
            dma((KV, 2, 7)),
            dma((KV, 2, n)),
            dma((KV, n)),
            dma((KV, n)),
            dma((2, n)),
            dma((2, n)),
            dma((2, inner)),
            dma((2, inner)),
            dma((2, outer)),
            dma((2, outer)),
        ],
        compiler_params=pltpu.CompilerParams(collective_id=0, has_side_effects=True, vmem_limit_bytes=VMEM_LIMIT),
        name="attend",
    )(start, bias, freqs, *(pltpu.with_memory_space_constraint(x[0], pltpu.HBM) for x in (q_proj, k_proj, v_proj, cache_k, cache_v, dout)))
    return (
        out[None], grad_q[None], grad_k[None], grad_v[None],
        total[:, :GROUP].reshape(HQ * HD), total[:, GROUP].reshape(KV * HD), total[:, GROUP + 1].reshape(KV * HD),
    )


VMEM_LIMIT = 44 << 20


def solution(mesh):
    n, m = mesh.shape["seq"], mesh.shape["dp"]
    tokens = P("dp", "seq", None)
    return jax.shard_map(
        functools.partial(body, n, m),
        mesh=mesh,
        in_specs=(tokens, tokens, tokens, tokens, tokens, P(), P(), P(), P("dp"), tokens),
        out_specs=(tokens, tokens, tokens, tokens, P(), P(), P()),
        check_vma=False,
    )
```

time: 99.2 us -> 94.8 us (0.956)
  local copies, waits for them, and re-layouts: 11.8 us -> 5.09 us
  Pallas kernels: 85.6 us -> 87.5 us
    unnamed x24 -> x6, local copies, waits for them, and re-layouts: 10.6 us -> 3.9 us
    pallas_call x1, Pallas kernels: 85.6 us -> 87.5 us  [body(): pl.pallas_call(functools.partial(attend_kernel, n, inner, outer), out_sha...]
where the time goes in v3:
time: 94.8 us; the launch traced here: 94.7 us
  Pallas kernels  87.5 us (92%)
  local copies, waits for them, and re-layouts  5.09 us (5%)
  between operations  1.3 us (1%)
    pallas_call x1, Pallas kernels, body(): pl.pallas_call(functools.partial(attend_kernel, n, inner, outer), out_sha...  87.5 us
    unnamed x6, local copies, waits for them, and re-layouts  3.9 us

profile of v3, /device:TPU:1, one launch (start us, length us, event | category | flops | bytes accessed | tf_op | source)
XLA Modules:
  0.0 94.7 jit_solution(15498902752745032532)
XLA Ops:
  0.6 0.7 fusion.bias_ref
  2.0 0.0 copy-start
  2.0 0.6 copy-done
  2.7 87.5 %attend.1 = (bf16[128,4096]{1,0:T(8,128)(2,1)S(1)}, bf16[128,4096]{1,0:T(8,128)(2,1)S(1)}, bf16[128,512]{1,0:T(8,128)(2,1)S(1)}, bf16[128,512]{1,0:T(8,128)(2,1)S(1)}, f32[4,16,128]{2,1,0:T(8,128)S(1)}) custom-call(s32[1]{0:T(128)S(6)} %copy.22.start_ref, f32[40,128]{1,0:T(8,128)S(1)} %fusion.bias_ref, f32[1,128]{1,0:T(1,128)S(1)} %copy-done, ...), custom_call_target="tpu_custom_call" | custom-call | tf_op jit(solution)/shard_map/attend/pallas_call | solution.py:466
  90.2 0.6 fusion.1
  90.8 0.6 slice_bitcast_fusion
  91.4 1.0 %copy.23 = bf16[1,128,4096]{2,1,0:T(8,128)(2,1)} copy(bf16[1,128,4096]{2,1,0:T(8,128)(2,1)S(1)} %bitcast.20) | data formatting | bytes 2097152
  92.4 1.0 %copy.24 = bf16[1,128,4096]{2,1,0:T(8,128)(2,1)} copy(bf16[1,128,4096]{2,1,0:T(8,128)(2,1)S(1)} %bitcast.19) | data formatting | bytes 2097152
  93.4 0.7 copy.25
  94.0 0.7 copy.26
Async XLA Ops:
  2.0 0.7 copy-start

commit v4 on v3

--- a/solution.py
+++ b/solution.py
@@ -14,6 +14,7 @@
 GROUP = 8
 SUMS = HQ + 2 * KV
 SLOTS = 16
+LOG_BASE = float(np.log(1e6))
 SCALE = float(HD**-0.5)
 EXP2_SCALE = float(np.log2(np.e) * HD**-0.5)
 MESH = pl.DeviceIdType.MESH
@@ -33,7 +34,7 @@
 
 def attend_kernel(
     n, inner, outer,
-    start_ref, bias_ref, freq_ref, q_ref, k_ref, v_ref, ck_ref, cv_ref, do_ref,
+    start_ref, bias_ref, q_ref, k_ref, v_ref, ck_ref, cv_ref, do_ref,
     out_ref, gq_ref, gk_ref, gv_ref, sums_ref,
     q_in, k_in, v_in, kv, rsend, rrecv, q_s, do_s, s_ref, p_ref, mask_ref, stat, norm, acc, q_t, do_t, do_n,
     cos_s, sin_s, sum_a, sum_b, sum_c,
@@ -103,10 +104,13 @@
 
     flip = jnp.where(lax.broadcasted_iota(jnp.int32, (1, HD), 1) < HD // 2, -1.0, 1.0)
 
+    pair = lax.rem(lax.broadcasted_iota(jnp.int32, (1, HD), 1), HD // 2).astype(f32)
+    freqs = jnp.exp(-(2.0 * pair / HD) * LOG_BASE)
+
     def table(owner):
         at = pl.ds(pl.multiple_of(owner * tokens, tokens), tokens)
         position = start_ref[0] + owner * tokens + lax.broadcasted_iota(jnp.int32, (tokens, HD), 0)
-        angle = position.astype(f32) * freq_ref[...]
+        angle = position.astype(f32) * freqs
         cos_s[at, :] = jnp.cos(angle)
         sin_s[at, :] = jnp.sin(angle) * flip
 
@@ -123,24 +127,23 @@
 
     pl.semaphore_wait(barrier, n + inner + outer - 3)
 
-    def kv_copy(h, part, owner, peer, slot):
-        block = kv.at[h, :, part, owner]
+    def kv_copy(h, half, part, owner, peer, slot):
+        block = kv.at[h, half, part, owner]
         return pltpu.make_async_remote_copy(
             src_ref=block, dst_ref=block,
-            send_sem=kv_send.at[h, part, slot], recv_sem=kv_recv.at[h, part, owner],
+            send_sem=kv_send.at[h, half, part, slot], recv_sem=kv_recv.at[h, half, part, owner],
             device_id={"seq": peer}, device_id_type=MESH,
         )
 
     top = ring - 1
-    routes = (
-        (me, side, jnp.logical_or(z == 0, y < top)),
-        (me, up, y < top),
-        (me, down, y == 0),
-        (side, up, y < top),
-        (side, down, y <= 1),
-        (down, up, jnp.logical_and(y >= 1, y < top)),
-        (side_up, down, jnp.logical_or(y == 0, y == top)),
-    )
+    to_side = jnp.logical_or(z == 0, y < top)
+    to_up = y < top
+    to_down = (y == 0, y <= 1)
+    pass_far = (jnp.logical_and(y >= 1, y < top), jnp.logical_or(y == 0, y == top))
+    from_side = jnp.logical_or(z == 1, y < top)
+    from_down = y >= 1
+    from_up = (y == top, jnp.logical_or(y == top, y == 0))
+    from_far = y >= 2
 
     def both_parts(needed, step):
         step(0)
@@ -149,47 +152,64 @@
         def _():
             step(1)
 
-    def send(h, *slots):
-        for slot in slots:
-            owner, peer, needed = routes[slot]
-            both_parts(needed, lambda part: kv_copy(h, part, owner, peer, slot).start())
-
-    def arrived(h, owner, needed):
-        both_parts(needed, lambda part: kv_copy(h, part, owner, owner, 0).wait_recv())
+    def send(h, half, owner, peer, slot, needed):
+        both_parts(needed, lambda part: kv_copy(h, half, part, owner, peer, slot).start())
+
+    def sent(h, half, peer, slot, needed):
+        both_parts(needed, lambda part: kv_copy(h, half, part, me, peer, slot).wait_send())
+
+    def arrived(h, half, owner, needed):
+        both_parts(needed, lambda part: kv_copy(h, half, part, owner, owner, 0).wait_recv())
 
     def send_own(h):
-        send(h, 0, 1, 2)
+        for half in range(2):
+            send(h, half, me, side, 0, to_side)
+            send(h, half, me, up, 1, to_up)
+            send(h, half, me, down, 2, to_down[half])
 
     def relay_near(h):
-        arrived(h, side, jnp.logical_or(z == 1, y < top))
-        send(h, 3, 4)
-        arrived(h, down, y >= 1)
-        send(h, 5)
+        for half in range(2):
+            arrived(h, half, side, from_side)
+            send(h, half, side, up, 3, to_up)
+            send(h, half, side, down, 4, to_down[half])
+            if half == 0:
+                arrived(h, 0, down, from_down)
+                send(h, 0, down, up, 5, pass_far[0])
+            else:
+                arrived(h, 1, up, from_up[1])
+                send(h, 1, up, down, 5, pass_far[1])
 
     def relay_far(h):
-        arrived(h, side_up, jnp.logical_or(y == top, y == 0))
-        send(h, 6)
-
-    def await_rest(h):
-        arrived(h, up, y == top)
-        arrived(h, side_down, y >= 1)
-        arrived(h, far, y >= 2)
-        arrived(h, side_far, y >= 2)
+        arrived(h, 0, side_down, from_down)
+        send(h, 0, side_down, up, 6, pass_far[0])
+        arrived(h, 1, side_up, from_up[1])
+        send(h, 1, side_up, down, 6, pass_far[1])
+
+    def await_half(h, half):
+        if half == 0:
+            arrived(h, 0, up, from_up[0])
+            arrived(h, 0, side_up, from_up[0])
+        else:
+            arrived(h, 1, down, from_down)
+            arrived(h, 1, side_down, from_down)
+        arrived(h, half, far, from_far)
+        arrived(h, half, side_far, from_far)
 
     def direct(step):
-        for part in range(2):
-
-            def one(i, _):
-                peer = lax.rem(me + i, n)
-                pl.when(jnp.logical_or(part == 0, peer > me))(lambda: step(kv_copy(0, part, me, peer, i - 1)))
-                return 0
-
-            lax.fori_loop(1, n, one, 0)
-
-    def await_direct():
+        for half in range(2):
+            for part in range(2):
+
+                def one(i, _):
+                    peer = lax.rem(me + i, n)
+                    pl.when(jnp.logical_or(part == 0, peer > me))(lambda: step(kv_copy(0, half, part, me, peer, i - 1)))
+                    return 0
+
+                lax.fori_loop(1, n, one, 0)
+
+    def await_direct(half):
         def one(i, _):
             owner = lax.rem(me + i, n)
-            arrived(0, owner, owner < me)
+            arrived(0, half, owner, owner < me)
             return 0
 
         lax.fori_loop(1, n, one, 0)
@@ -295,11 +315,11 @@
 
         @pl.when(h == 0)
         def _():
-            await_direct()
+            await_direct(0)
 
         @pl.when(h > 0)
         def _():
-            await_rest(h)
+            await_half(h, 0)
 
         q_t[...] = q_s[h].T
         stat[...] = jnp.full(stat.shape, -3e38, f32)
@@ -314,7 +334,8 @@
             stat[...] = m
             return 0
 
-        lax.fori_loop(0, 2, score, 0)
+        for part in range(2):
+            score(part, 0)
 
         @pl.when(h + 1 < KV)
         def _():
@@ -324,6 +345,15 @@
         stat[...] = jnp.broadcast_to(jnp.max(stat[...], axis=1, keepdims=True), stat.shape)
         norm[...] = jnp.zeros(norm.shape, f32)
         acc[...] = jnp.zeros(acc.shape, f32)
+
+        @pl.when(h == 0)
+        def _():
+            await_direct(1)
+
+        @pl.when(h > 0)
+        def _():
+            await_half(h, 1)
+
 
         def weigh(part, _):
             m = stat[...]
@@ -429,8 +459,15 @@
     begin_c(1)
 
     def drain_head(h, _):
-        for slot, (_owner, peer, needed) in enumerate(routes):
-            both_parts(needed, lambda part: kv_copy(h, part, me, peer, slot).wait_send())
+        for half in range(2):
+            for slot, (peer, needed) in enumerate(
+                (
+                    (side, to_side), (up, to_up), (down, to_down[half]), (up, to_up), (down, to_down[half]),
+                    (up if half == 0 else down, pass_far[half]), (up if half == 0 else down, pass_far[half]),
+                )
+            ):
+                sent(h, half, peer, slot, needed)
+
         return 0
 
     def drain_back(h, _):
@@ -452,14 +489,21 @@
     leave_c(1)
 
 
+def store_kernel(*refs):
+    count = len(refs) // 2
+    sources, targets, sem = refs[:count], refs[count : 2 * count], refs[-1]
+    copies = [pltpu.make_async_copy(a, b, sem.at[i]) for i, (a, b) in enumerate(zip(sources, targets))]
+    for copy in copies:
+        copy.start()
+    for copy in copies:
+        copy.wait()
+
+
 def body(n, m, q_proj, k_proj, v_proj, cache_k, cache_v, bias_q, bias_k, bias_v, start, dout):
     tokens = q_proj.shape[1]
     keys, rows = n * tokens, GROUP * tokens
     inner = 8
     outer = m // inner
-    half = HD // 2
-    freqs = np.exp(-(2.0 * np.arange(half) / HD) * np.log(1e6)).astype(np.float32)
-    freqs = jnp.asarray(np.concatenate([freqs, freqs])[None])
     bias = jnp.concatenate([bias_q, bias_k, bias_v]).astype(f32).reshape(SUMS, HD)
     vmem = pl.BlockSpec(memory_space=pltpu.VMEM)
     dma = pltpu.SemaphoreType.DMA
@@ -472,7 +516,7 @@
             jax.ShapeDtypeStruct((tokens, KV * HD), bf16),
             jax.ShapeDtypeStruct((KV, SLOTS, HD), f32),
         ],
-        in_specs=[pl.BlockSpec(memory_space=pltpu.SMEM), vmem, vmem] + [pl.BlockSpec(memory_space=pltpu.HBM)] * 6,
+        in_specs=[pl.BlockSpec(memory_space=pltpu.SMEM), vmem] + [pl.BlockSpec(memory_space=pltpu.HBM)] * 6,
         out_specs=[vmem] * 5,
         scratch_shapes=[
             pltpu.VMEM((tokens, HQ * HD), bf16),
@@ -500,8 +544,8 @@
             dma((3,)),
             dma((KV, 2)),
             dma((KV, GROUP)),
-            dma((KV, 2, 7)),
-            dma((KV, 2, n)),
+            dma((KV, 2, 2, 7)),
+            dma((KV, 2, 2, n)),
             dma((KV, n)),
             dma((KV, n)),
             dma((2, n)),
@@ -513,9 +557,19 @@
         ],
         compiler_params=pltpu.CompilerParams(collective_id=0, has_side_effects=True, vmem_limit_bytes=VMEM_LIMIT),
         name="attend",
-    )(start, bias, freqs, *(pltpu.with_memory_space_constraint(x[0], pltpu.HBM) for x in (q_proj, k_proj, v_proj, cache_k, cache_v, dout)))
+    )(start, bias, *(pltpu.with_memory_space_constraint(x[0], pltpu.HBM) for x in (q_proj, k_proj, v_proj, cache_k, cache_v, dout)))
+    anywhere, hbm = pl.BlockSpec(memory_space=pl.ANY), pl.BlockSpec(memory_space=pltpu.HBM)
+    results = pl.pallas_call(
+        store_kernel,
+        out_shape=[jax.ShapeDtypeStruct(x.shape, x.dtype) for x in (out, grad_q, grad_k, grad_v)],
+        in_specs=[anywhere] * 4,
+        out_specs=[hbm] * 4,
+        scratch_shapes=[dma((4,))],
+        compiler_params=pltpu.CompilerParams(vmem_limit_bytes=1 << 20),
+        name="store",
+    )(out, grad_q, grad_k, grad_v)
     return (
-        out[None], grad_q[None], grad_k[None], grad_v[None],
+        *(x[None] for x in results),
         total[:, :GROUP].reshape(HQ * HD), total[:, GROUP].reshape(KV * HD), total[:, GROUP + 1].reshape(KV * HD),
     )
 

time: 94.8 us -> 89.8 us (0.947)
  local copies, waits for them, and re-layouts: 5.09 us -> 1.87 us
  Pallas kernels: 87.5 us -> 86.4 us
    unnamed x6, local copies, waits for them, and re-layouts: 3.9 us -> 0.68 us
    pallas_call x1, Pallas kernels: 87.5 us -> 85 us  [body(): pl.pallas_call(functools.partial(attend_kernel, n, inner, outer), out_sha...]
    pallas_call x0 -> x1, Pallas kernels: none -> 1.43 us  [body(): pl.pallas_call(store_kernel, out_shape=[jax.ShapeDtypeStruct(x.shape, x.d...]
where the time goes in v4:
time: 89.8 us; the launch traced here: 89.6 us
  Pallas kernels  86.4 us (96%)
  local copies, waits for them, and re-layouts  1.87 us (2%)
  between operations  1.34 us (1%)
    pallas_call x1, Pallas kernels, body(): pl.pallas_call(functools.partial(attend_kernel, n, inner, outer), out_sha...  85 us

profile of v4, /device:TPU:1, one launch (start us, length us, event | category | flops | bytes accessed | tf_op | source)
XLA Modules:
  0.0 89.6 jit_solution(9742196385555108997)
XLA Ops:
  0.6 0.0 copy-start
  1.3 0.0 copy-start.2
  1.3 0.0 copy-start.1
  1.3 0.0 copy-done
  1.3 0.7 copy-done.2
  2.0 0.0 copy-done.1
  2.0 85.0 %attend.1 = (bf16[128,4096]{1,0:T(8,128)(2,1)S(1)}, bf16[128,4096]{1,0:T(8,128)(2,1)S(1)}, bf16[128,512]{1,0:T(8,128)(2,1)S(1)}, bf16[128,512]{1,0:T(8,128)(2,1)S(1)}, f32[4,16,128]{2,1,0:T(8,128)S(1)}) custom-call(s32[1]{0:T(128)S(6)} %copy.17.start_ref, f32[40,128]{1,0:T(8,128)S(1)} %fusion.bias_ref, bf16[128,4096]{1,0:T(8,128)(2,1)} %bitcast.19, ...), custom_call_target="tpu_custom_call" | custom-call | tf_op jit(solution)/shard_map/attend/pallas_call | solution.py:510
  87.0 1.4 %store.1 = (bf16[128,4096]{1,0:T(8,128)(2,1)}, bf16[128,4096]{1,0:T(8,128)(2,1)}, bf16[128,512]{1,0:T(8,128)(2,1)}, bf16[128,512]{1,0:T(8,128)(2,1)}) custom-call(bf16[128,4096]{1,0:T(8,128)(2,1)S(1)} %get-tuple-element.16.refs_0_, bf16[128,4096]{1,0:T(8,128)(2,1)S(1)} %get-tuple-element.17.refs_1_, bf16[128,512]{1,0:T(8,128)(2,1)S(1)} %get-tuple-element.18.refs_2_, ...), custom_call_target="tpu_custom_call" | custom-call | tf_op jit(solution)/shard_map/store/pallas_call | solution.py:562
  88.4 0.6 fusion.1
  89.0 0.6 slice_bitcast_fusion
  (1 shorter events, 0.0 us)
Async XLA Ops:
  0.6 0.7 copy-start
  1.3 0.7 copy-start.2
  1.3 0.7 copy-start.1

commit v5 on v4

--- a/solution.py
+++ b/solution.py
@@ -195,16 +195,15 @@
         arrived(h, half, far, from_far)
         arrived(h, half, side_far, from_far)
 
-    def direct(step):
-        for half in range(2):
-            for part in range(2):
-
-                def one(i, _):
-                    peer = lax.rem(me + i, n)
-                    pl.when(jnp.logical_or(part == 0, peer > me))(lambda: step(kv_copy(0, half, part, me, peer, i - 1)))
-                    return 0
-
-                lax.fori_loop(1, n, one, 0)
+    def direct(half, step):
+        for part in range(2):
+
+            def one(i, _):
+                peer = lax.rem(me + i, n)
+                pl.when(jnp.logical_or(part == 0, peer > me))(lambda: step(kv_copy(0, half, part, me, peer, i - 1)))
+                return 0
+
+            lax.fori_loop(1, n, one, 0)
 
     def await_direct(half):
         def one(i, _):
@@ -234,8 +233,7 @@
         return 0
 
     lax.fori_loop(0, KV, await_cache, 0)
-    direct(lambda copy: copy.start())
-    send_own(1)
+    direct(0, lambda copy: copy.start())
 
     def begin_do(i, _):
         fetch_do(i // GROUP, lax.rem(i, GROUP)).start()
@@ -244,6 +242,8 @@
     lax.fori_loop(0, KV * GROUP, begin_do, 0)
     fetch_q.wait()
     lax.fori_loop(0, KV, load_queries, 0)
+    direct(1, lambda copy: copy.start())
+    send_own(1)
 
     row = lax.broadcasted_iota(jnp.int32, (tokens, keys), 0)
     col = lax.broadcasted_iota(jnp.int32, (tokens, keys), 1)
@@ -343,8 +343,6 @@
 
 
         stat[...] = jnp.broadcast_to(jnp.max(stat[...], axis=1, keepdims=True), stat.shape)
-        norm[...] = jnp.zeros(norm.shape, f32)
-        acc[...] = jnp.zeros(acc.shape, f32)
 
         @pl.when(h == 0)
         def _():
@@ -355,16 +353,21 @@
             await_half(h, 1)
 
 
-        def weigh(part, _):
-            m = stat[...]
-            pieces = [
-                jnp.exp2((s_ref[part, :, t * HD : (t + 1) * HD] - m) * EXP2_SCALE)
-                for t in range(keys // HD)
-            ]
-            norm[...] += functools.reduce(lambda a, b: a + b, pieces)
-            p = jnp.concatenate([x.astype(bf16) for x in pieces], axis=1)
-            p_ref[part] = p
-            acc[...] += dot(p, kv[h, 1, part].reshape(keys, HD), 1, 0)
+        def weigh(i, _):
+            at = pl.ds(pl.multiple_of(i * (rows // 2), rows // 2), rows // 2)
+            m = stat[at, :]
+            total, product = 0.0, 0.0
+            for part in range(2):
+                pieces = [
+                    jnp.exp2((s_ref[part, at, t * HD : (t + 1) * HD] - m) * EXP2_SCALE)
+                    for t in range(keys // HD)
+                ]
+                total += functools.reduce(lambda a, b: a + b, pieces)
+                p = jnp.concatenate([x.astype(bf16) for x in pieces], axis=1)
+                p_ref[part, at, :] = p
+                product += dot(p, kv[h, 1, part].reshape(keys, HD), 1, 0)
+            norm[at, :] = total
+            acc[at, :] = product
             return 0
 
         lax.fori_loop(0, 2, weigh, 0)
@@ -441,7 +444,7 @@
         filler = jnp.zeros((SLOTS - GROUP - 2, HD), f32)
         sum_a[me, h] = jnp.concatenate(sums + key_sums + [filler], axis=0)
 
-        @pl.when(h > 0)
+        @pl.when(jnp.logical_and(h > 0, h + 1 < KV))
         def _():
             finish(h - 1)
 
@@ -450,6 +453,7 @@
     lax.fori_loop(0, KV, head, 0)
 
     begin_a(1)
+    finish(KV - 2)
     sum_c[block, early] = arrive_b(0)
     begin_c(0)
     sum_b[lane, late] = arrive_a(1)
@@ -477,7 +481,8 @@
 
         return lax.fori_loop(0, me, one, 0)
 
-    direct(lambda copy: copy.wait_send())
+    direct(0, lambda copy: copy.wait_send())
+    direct(1, lambda copy: copy.wait_send())
     lax.fori_loop(1, KV, drain_head, 0)
     lax.fori_loop(0, KV, drain_back, 0)
     for which in range(2):

time: 89.8 us -> 89.5 us (level)
  no operation moved by 1% of the time
where the time goes in v5:
time: 89.5 us; the launch traced here: 89.4 us
  Pallas kernels  86.2 us (96%)
  local copies, waits for them, and re-layouts  1.87 us (2%)
  between operations  1.34 us (1%)
    pallas_call x1, Pallas kernels, body(): pl.pallas_call(functools.partial(attend_kernel, n, inner, outer), out_sha...  84.7 us

profile of v5, /device:TPU:1, one launch (start us, length us, event | category | flops | bytes accessed | tf_op | source)
XLA Modules:
  0.0 89.4 jit_solution(4242249161026408176)
XLA Ops:
  0.6 0.0 copy-start
  1.3 0.0 copy-start.2
  1.3 0.0 copy-start.1
  1.3 0.0 copy-done
  1.3 0.7 copy-done.2
  2.0 0.0 copy-done.1
  2.0 84.7 %attend.1 = (bf16[128,4096]{1,0:T(8,128)(2,1)S(1)}, bf16[128,4096]{1,0:T(8,128)(2,1)S(1)}, bf16[128,512]{1,0:T(8,128)(2,1)S(1)}, bf16[128,512]{1,0:T(8,128)(2,1)S(1)}, f32[4,16,128]{2,1,0:T(8,128)S(1)}) custom-call(s32[1]{0:T(128)S(6)} %copy.17.start_ref, f32[40,128]{1,0:T(8,128)S(1)} %fusion.bias_ref, bf16[128,4096]{1,0:T(8,128)(2,1)} %bitcast.19, ...), custom_call_target="tpu_custom_call" | custom-call | tf_op jit(solution)/shard_map/attend/pallas_call | solution.py:515
  86.7 1.4 %store.1 = (bf16[128,4096]{1,0:T(8,128)(2,1)}, bf16[128,4096]{1,0:T(8,128)(2,1)}, bf16[128,512]{1,0:T(8,128)(2,1)}, bf16[128,512]{1,0:T(8,128)(2,1)}) custom-call(bf16[128,4096]{1,0:T(8,128)(2,1)S(1)} %get-tuple-element.16.refs_0_, bf16[128,4096]{1,0:T(8,128)(2,1)S(1)} %get-tuple-element.17.refs_1_, bf16[128,512]{1,0:T(8,128)(2,1)S(1)} %get-tuple-element.18.refs_2_, ...), custom_call_target="tpu_custom_call" | custom-call | tf_op jit(solution)/shard_map/store/pallas_call | solution.py:567
  88.2 0.6 fusion.1
  88.8 0.6 slice_bitcast_fusion
  (1 shorter events, 0.0 us)
Async XLA Ops:
  0.6 0.7 copy-start
  1.3 0.7 copy-start.2
  1.3 0.7 copy-start.1
